TPU v7x, 32 devices: a whole 2x2x4 slice. The times are simulated.
32 devices in a mesh: groups: 2 (over y), seq: 4 (over z), mp: 4 (over x, core).
Axes of the slice: x: 2, y: 2, z: 4, core: 2. Of those that a mesh axis runs over, the one named last changes fastest.
Arguments:
- points: bfloat16 [131072, 256], P(('groups', 'seq'), 'mp'), parts along dimension 0, may hold values from -6 to 6
- w_query: bfloat16 [256, 256], replicated, may hold values from -2 to 2
- w_key: bfloat16 [256, 256], replicated, may hold values from -2 to 2
- w_value: bfloat16 [256, 256], replicated, may hold values from -0.375 to 0.375
- w_out: bfloat16 [256, 256], replicated, may hold values from -0.375 to 0.375
- w_up: bfloat16 [256, 1024], replicated, may hold values from -0.375 to 0.375
- w_down: bfloat16 [1024, 256], replicated, may hold values from -0.1875 to 0.1875
- w_pool: bfloat16 [2048, 512], replicated, may hold values from -0.125 to 0.125
- keep_count: int32 [32], P(('groups', 'seq', 'mp')), parts along dimension 0, may hold values from 0 to 32, as said below
Outputs:
- refined: bfloat16 [131072, 256], P(('groups', 'seq', 'mp')), parts along dimension 0
- coarse: bfloat16 [32768, 512], P(('groups', 'seq', 'mp')), parts along dimension 0
There are 2 independent parts, one for each index of `groups`. A program takes and returns all parts, laid end to end along the dimension named above; an argument that names none is the same for every part. Nothing has to cross between parts.
Inputs may be any that keep to these rules, and one draw needn't show every extreme that they name: `keep_count`: in every draw some block keeps 0 tiles and some block keeps all 32.
All inputs are finite; a program needn't handle non-finite values.
Results may differ from a plain program's by a relative error of at most 0.0061.
Values may be sent and summed in bfloat16 or wider, within the bound.
No kernel may reach another device: no remote copies, remote signals or barrier semaphores. Data moves between devices by JAX's collectives and lax.ppermute only.
A program may use at most 192 MiB of HBM per device.

v0:
```python
import functools
import math

import jax
import jax.numpy as jnp
import numpy as np
from jax import lax
from jax.experimental import pallas as pl
from jax.experimental.pallas import tpu as pltpu
from jax.sharding import PartitionSpec as P

HEADS = 8
WINDOW = 32
DILATION = 4
TILE_PARENTS = 16
CHILDREN = 8
BLOCK = WINDOW * DILATION
HALF = BLOCK // 2
STEP = 3
CHUNK_STEPS = (3, 3, 3, 2)

BF = jnp.bfloat16
F32 = jnp.float32


def gather_order():
    place = np.zeros((BLOCK, 2 * BLOCK), np.float32)
    for r in range(DILATION):
        for j in range(WINDOW):
            place[r * WINDOW + j, HALF + DILATION * j + r] = 1.0
    return place


def output_order():
    back = np.zeros((2 * BLOCK, BLOCK), np.float32)
    for r in range(DILATION):
        for j in range(WINDOW):
            p = DILATION * j + r
            back[p, r * WINDOW + j] = 1.0
            back[BLOCK + (p % CHILDREN) * TILE_PARENTS + p // CHILDREN, r * WINDOW + j] = 1.0
    return back


def head_masks(width):
    size = width // HEADS
    half = WINDOW // 2
    rows = np.arange(HEADS * half)[:, None] // half
    cols = np.arange(width)[None, :] // size
    mask = (rows == cols).astype(np.float32)
    return np.concatenate([mask, mask], axis=0)


def norm_rows(values):
    centre = values - jnp.mean(values, axis=-1, keepdims=True)
    spread = jnp.mean(centre * centre, axis=-1, keepdims=True)
    return centre * lax.rsqrt(spread + 1e-05)


def dot_nn(a, b):
    return lax.dot_general(a, b, (((1,), (0,)), ((), ())), preferred_element_type=F32)


def dot_nt(a, b):
    return lax.dot_general(a, b, (((1,), (1,)), ((), ())), preferred_element_type=F32)


def segment_max(scores):
    width = scores.shape[1] // 2
    run = WINDOW // 2
    top = jnp.maximum(scores[:, :width], scores[:, width:])
    for shift in (1, 2, 4, 8):
        top = jnp.maximum(top, pltpu.roll(top, shift, 1))
    lane = lax.broadcasted_iota(jnp.int32, top.shape, 1)
    top = jnp.where(lane % run == run - 1, top, -jnp.inf)
    for shift in (1, 2, 4, 8):
        top = jnp.maximum(top, pltpu.roll(top, width - shift, 1))
    return top


def layer_step(x, w, win_count):
    width = x.shape[1]
    normed = norm_rows(x).astype(BF)
    qkv = dot_nn(normed, w["qkv"][...]).astype(BF)
    mask = w["mask"][...]
    run = WINDOW // 2
    groups = win_count * DILATION
    scores = []
    for g in range(groups):
        rows = slice(g * WINDOW, (g + 1) * WINDOW)
        q = qkv[rows, :width]
        k = qkv[rows, width : 2 * width]
        wide = jnp.concatenate([k[:run]] * HEADS + [k[run:]] * HEADS, axis=0) * mask
        scores.append(dot_nt(q, wide))
    scores = jnp.concatenate(scores, axis=0)
    top = segment_max(scores)
    top = jnp.concatenate([top, top], axis=1)
    factor = math.log2(math.e) / math.sqrt(width // HEADS)
    weights = jnp.exp2((scores - top) * factor).astype(BF)
    total = dot_nn(weights, mask)
    mixed = []
    for g in range(groups):
        rows = slice(g * WINDOW, (g + 1) * WINDOW)
        v = qkv[rows, 2 * width :]
        wide = jnp.concatenate([v[:run]] * HEADS + [v[run:]] * HEADS, axis=0) * mask
        mixed.append(dot_nn(weights[rows], wide))
    attended = (jnp.concatenate(mixed, axis=0) / total).astype(BF)
    hidden = x + dot_nn(attended, w["out"][...])
    normed_two = norm_rows(hidden).astype(BF)
    up = dot_nn(normed_two, w["up"][...])
    inner = up * (0.7978845608028654 + 0.035677408136300125 * (up * up))
    activated = (0.5 * up * (1.0 + jnp.tanh(inner))).astype(BF)
    return (hidden + dot_nn(activated, w["down"][...])).astype(BF)


def chunk_kernel(spec, *refs):
    first_tile, tiles, first_window, steps, last, aliased, quarter, feat = spec
    names = ["place", "own"]
    n_recv = 3
    it = iter(refs)
    place_ref = next(it)
    own = next(it)
    recv = [next(it) for _ in range(n_recv)]
    if first_window > 1:
        before = [next(it) for _ in range(n_recv)]
    if last:
        halo_own = next(it)
        start = [next(it) for _ in range(n_recv)]
    hbm = {k: next(it) for k in ("gather", "mask", "qkv", "out", "up", "down", "back", "pool")}
    if aliased:
        next(it)
    refined, pooled = next(it), next(it)
    xbuf, ybuf, pbuf = next(it), next(it), next(it)
    w = {k: next(it) for k in ("gather", "mask", "qkv", "out", "up", "down", "back", "pool")}
    pooled_buf = next(it)
    in_sem, w_sem, out_sem, pool_sem = next(it), next(it), next(it), next(it)
    mp_index = place_ref[0]
    copies = []

    def bring(src, source_shift, col, width):
        j = lax.rem(mp_index + 4 - source_shift, 4)
        dst = xbuf.at[pl.ds(pl.multiple_of(j * feat, feat), feat), pl.ds(col, width)]
        c = pltpu.make_async_copy(src, dst, in_sem.at[len(copies)])
        c.start()
        copies.append(c)

    def own_cols(tile, count):
        return own.at[:, pl.ds(pl.multiple_of(mp_index * quarter + tile * BLOCK, BLOCK), count * BLOCK)]

    lead = 0
    if first_window > 1:
        lead = 1
        for s in range(n_recv):
            n_before = before[s].shape[1]
            bring(before[s].at[:, pl.ds(n_before - BLOCK, BLOCK)], s + 1, 0, BLOCK)
        bring(own_cols(first_tile - 1, 1), 0, 0, BLOCK)
    for s in range(n_recv):
        bring(recv[s], s + 1, lead * BLOCK, recv[s].shape[1])
    bring(own_cols(first_tile, tiles), 0, lead * BLOCK, tiles * BLOCK)
    if last:
        bring(halo_own, 0, (lead + tiles) * BLOCK, BLOCK)
        for s in range(n_recv):
            bring(start[s].at[:, pl.ds(0, BLOCK)], s + 1, (lead + tiles + 1) * BLOCK, BLOCK)
        bring(own_cols(0, 1), 0, (lead + tiles + 1) * BLOCK, BLOCK)
    loads = {}
    for n, key in enumerate(hbm):
        loads[key] = pltpu.make_async_copy(hbm[key], w[key], w_sem.at[n])
        loads[key].start()
    for c in copies:
        c.wait()
    for key in hbm:
        if key != "pool":
            loads[key].wait()

    rows_step = STEP * BLOCK
    windows = steps * STEP
    width = 4 * feat

    def step(s, carry):
        gather = w["gather"][...]
        xs = []
        for n in range(STEP):
            col = pl.multiple_of((s * STEP + n) * BLOCK, BLOCK)
            xs.append(dot_nt(gather, xbuf[:, pl.ds(col, 2 * BLOCK)]))
        ys = layer_step(jnp.concatenate(xs, axis=0), w, STEP)
        back = w["back"][...]
        for n in range(STEP):
            both = dot_nn(back, ys[n * BLOCK : (n + 1) * BLOCK]).astype(BF)
            row = pl.multiple_of((s * STEP + n) * BLOCK, BLOCK)
            ybuf[pl.ds(row, BLOCK), :] = both[:BLOCK]
            parent = pl.multiple_of((s * STEP + n) * TILE_PARENTS, TILE_PARENTS)
            for c in range(CHILDREN):
                piece = both[BLOCK + c * TILE_PARENTS : BLOCK + (c + 1) * TILE_PARENTS]
                pbuf[pl.ds(parent, TILE_PARENTS), c * width : (c + 1) * width] = piece
        return carry

    lax.fori_loop(0, steps, step, 0)
    base = first_window * BLOCK - HALF
    outs = []
    if last:
        rows = quarter - base
        outs.append(pltpu.make_async_copy(ybuf.at[pl.ds(0, rows)], refined.at[pl.ds(base, rows)], out_sem.at[0]))
        outs.append(
            pltpu.make_async_copy(
                ybuf.at[pl.ds(windows * BLOCK - HALF, HALF)], refined.at[pl.ds(0, HALF)], out_sem.at[1]
            )
        )
    else:
        rows = windows * BLOCK
        outs.append(pltpu.make_async_copy(ybuf, refined.at[pl.ds(base, rows)], out_sem.at[0]))
    for c in outs:
        c.start()
    loads["pool"].wait()
    result = dot_nn(pbuf[...], w["pool"][...])
    pooled_buf[...] = result.reshape(pooled_buf.shape).astype(BF)
    c = pltpu.make_async_copy(pooled_buf, pooled, pool_sem.at[0])
    c.start()
    c.wait()
    for c in outs:
        c.wait()


def run_chunk(spec, mp_index, own, recv, before, halo_own, start, weights, refined, rows, pool_width):
    first_tile, tiles, first_window, steps, last, aliased, quarter, feat = spec
    windows = steps * STEP
    width = 4 * feat
    args = [mp_index, own] + recv
    if first_window > 1:
        args += before
    if last:
        args += [halo_own] + start
    keys = ("gather", "mask", "qkv", "out", "up", "down", "back", "pool")
    args += [weights[k] for k in keys]
    aliases = {}
    if aliased:
        aliases = {len(args): 0}
        args.append(refined)
    any_spec = pl.BlockSpec(memory_space=pl.ANY)
    in_specs = [pl.BlockSpec(memory_space=pltpu.SMEM)] + [any_spec] * (len(args) - 1)
    halves = windows * TILE_PARENTS // 8
    scratch = [
        pltpu.VMEM((width, (windows + 1) * BLOCK), BF),
        pltpu.VMEM((windows * BLOCK, width), BF),
        pltpu.VMEM((windows * TILE_PARENTS, CHILDREN * width), BF),
    ]
    scratch += [pltpu.VMEM(weights[k].shape, BF) for k in keys]
    scratch += [
        pltpu.VMEM((halves, 8, pool_width), BF),
        pltpu.SemaphoreType.DMA((16,)),
        pltpu.SemaphoreType.DMA((len(keys),)),
        pltpu.SemaphoreType.DMA((2,)),
        pltpu.SemaphoreType.DMA((1,)),
    ]
    points = windows * BLOCK
    flops = 2 * points * (width * width * 16 + 2 * width * weights["up"].shape[1] + width * pool_width)
    return pl.pallas_call(
        functools.partial(chunk_kernel, spec),
        out_shape=(
            jax.ShapeDtypeStruct((rows, width), BF),
            jax.ShapeDtypeStruct((halves, 8, pool_width), BF),
        ),
        in_specs=in_specs,
        out_specs=(any_spec, any_spec),
        scratch_shapes=scratch,
        input_output_aliases=aliases,
        compiler_params=pltpu.CompilerParams(vmem_limit_bytes=48 << 20),
        cost_estimate=pl.CostEstimate(
            flops=flops, transcendentals=points * 1024, bytes_accessed=points * width * 4 + (4 << 20)
        ),
        name=f"layer_chunk_{first_window}",
    )(*args)


def place_kernel(counts, *refs):
    n = (len(refs) - 2) // 2
    own, came, out, zero = refs[:n], refs[n : 2 * n], refs[2 * n], refs[2 * n + 1]
    del zero
    slots = out.shape[0]
    total = slots // 2
    kept = counts[0] * 2
    kept_before = counts[1] * 2
    blank = jnp.zeros(out.shape[1:], BF)

    def clear(v, carry):
        out[v] = blank
        return carry

    lax.fori_loop(kept + total - kept_before, slots, clear, 0)
    lower = 1
    for n_piece in range(n):
        count = own[n_piece].shape[0]
        upper = min(lower + count, total)

        def keep(v, carry, piece=own[n_piece], low=lower):
            out[v] = piece[v - low]
            return carry

        def take(v, carry, piece=came[n_piece], low=lower):
            out[v + kept - kept_before] = piece[v - low]
            return carry

        lax.fori_loop(lower, jnp.minimum(kept, upper), keep, 0)
        lax.fori_loop(jnp.maximum(kept_before, lower), upper, take, 0)
        lower += count
    last = own[n - 1].shape[0] - 1

    @pl.when(kept > 0)
    def _():
        out[0] = own[n - 1][last]

    @pl.when(kept_before == 0)
    def _():
        out[kept] = came[n - 1][last]


def body(points, w_query, w_key, w_value, w_out, w_up, w_down, w_pool, keep_count):
    width = w_out.shape[0]
    feat = points.shape[1]
    ways = lax.axis_size("mp")
    seq_ways = lax.axis_size("seq")
    quarter = points.shape[0] // ways
    pool_width = w_pool.shape[1]
    mp_index = lax.axis_index("mp").astype(jnp.int32)
    own = points.T
    tiles_all = own.shape[1] // BLOCK
    tiles_quarter = quarter // BLOCK

    first = own[:, :BLOCK]
    final = own[:, own.shape[1] - BLOCK :]
    after = lax.ppermute(first, "seq", [((i + 1) % seq_ways, i) for i in range(seq_ways)])
    prior = lax.ppermute(final, "seq", [(i, (i + 1) % seq_ways) for i in range(seq_ways)])

    chunk_tiles = []
    tile = 0
    for n, steps in enumerate(CHUNK_STEPS):
        count = steps * STEP
        if n == 0:
            count += 1
        if n == len(CHUNK_STEPS) - 1:
            count = tiles_quarter - tile
        chunk_tiles.append((tile, count))
        tile += count

    head = jnp.stack([own[:, q * quarter : q * quarter + BLOCK] for q in range(1, ways)] + [after])
    tail = jnp.stack([prior] + [own[:, q * quarter - BLOCK : q * quarter] for q in range(1, ways)])
    lane = lax.broadcasted_iota(jnp.int32, (1, 1, BLOCK), 2)
    halos = jnp.where(lane < HALF, head, tail)
    halo_own = lax.dynamic_index_in_dim(halos, mp_index, 0, keepdims=False)

    received = []
    for n, (tile, count) in enumerate(chunk_tiles):
        got = []
        for s in (1, 2, 3):
            dest = (mp_index + s) % ways
            block = lax.dynamic_slice_in_dim(own, dest * quarter + tile * BLOCK, count * BLOCK, 1)
            if n == len(chunk_tiles) - 1:
                halo = lax.dynamic_index_in_dim(halos, dest, 0, keepdims=False)
                block = jnp.concatenate([block, halo], axis=1)
            got.append(lax.ppermute(block, "mp", [(i, (i + s) % ways) for i in range(ways)]))
        received.append(got)

    weights = {
        "gather": jnp.asarray(gather_order(), BF),
        "mask": jnp.asarray(head_masks(width), BF),
        "qkv": jnp.concatenate([w_query, w_key, w_value], axis=1),
        "out": w_out,
        "up": w_up,
        "down": w_down,
        "back": jnp.asarray(output_order(), BF),
        "pool": w_pool,
    }
    pairs = [(i, (i + 1) % (seq_ways * ways)) for i in range(seq_ways * ways)]
    kept_before = lax.ppermute(keep_count, ("seq", "mp"), pairs)
    refined = None
    window = 1
    own_pooled, came_pooled = [], []
    for n, steps in enumerate(CHUNK_STEPS):
        tile, count = chunk_tiles[n]
        last = n == len(CHUNK_STEPS) - 1
        spec = (tile, count, window, steps, last, n > 0, quarter, feat)
        refined, pooled = run_chunk(
            spec,
            mp_index[None],
            own,
            received[n],
            received[n - 1] if n else None,
            halo_own,
            received[0],
            weights,
            refined,
            quarter,
            pool_width,
        )
        own_pooled.append(pooled)
        came_pooled.append(lax.ppermute(pooled, ("seq", "mp"), pairs))
        window += steps * STEP

    counts = jnp.concatenate([keep_count, kept_before])
    slots = 2 * quarter // (CHILDREN * 8)
    vmem = pl.BlockSpec(memory_space=pltpu.VMEM)
    coarse = pl.pallas_call(
        place_kernel,
        out_shape=jax.ShapeDtypeStruct((slots, 8, pool_width), BF),
        in_specs=[pl.BlockSpec(memory_space=pltpu.SMEM)] + [vmem] * (2 * len(CHUNK_STEPS)),
        out_specs=vmem,
        scratch_shapes=[pltpu.VMEM((8, pool_width), BF)],
        compiler_params=pltpu.CompilerParams(vmem_limit_bytes=32 << 20),
        name="place_tiles",
    )(counts, *own_pooled, *came_pooled)
    return (refined, coarse.reshape(slots * 8, pool_width))


def solution(mesh):
    placed = (
        P(("groups", "seq"), "mp"),
        P(),
        P(),
        P(),
        P(),
        P(),
        P(),
        P(),
        P(("groups", "seq", "mp")),
    )
    return jax.shard_map(
        body,
        mesh=mesh,
        in_specs=placed,
        out_specs=(P(("groups", "seq", "mp"), None), P(("groups", "seq", "mp"), None)),
        check_vma=False,
    )
```

profile of v0, /device:TPU:0, one launch (start us, length us, event | category | flops | bytes accessed | tf_op | source)
XLA Modules:
  0.0 88.7 jit_solution(2356823843581572931)
XLA Ops:
  0.6 0.0 copy-start
  0.7 2.0 %dynamic-slice_bitcast_fusion = (bf16[64,1280]{1,0:T(8,128)(2,1)}, bf16[64,1280]{1,0:T(8,128)(2,1)}, bf16[64,1280]{1,0:T(8,128)(2,1)}) fusion(bf16[16384,64]{0,1:T(8,128)(2,1)} %param.12, s32[]{:T(128)S(6)} %select_n.102, s32[]{:T(128)S(6)} %select_n.101, s32[]{:T(128)S(6)} %select_n.100), kind=kLoop, calls=%fused_computation | loop fusion | bytes 983052 | tf_op jit(solution)/shard_map/dynamic_slice | solution.py:354
  2.7 2.4 %collective-permute-start.10 = (bf16[64,1280]{1,0:T(8,128)(2,1)}, bf16[64,1280]{1,0:T(8,128)(2,1)}, u32[]{:S(2)}, u32[]{:S(2)}) collective-permute-start(bf16[64,1280]{1,0:T(8,128)(2,1)} %get-tuple-element.24), channel_id=1, source_target_pairs={{0,3},{1,0},{2,1},{3,2},{4,7},{5,4},{6,5},{7,6},{8,11},{9,8},{10,9... | collective-permute-start | bytes 491528 | tf_op jit(solution)/shard_map/ppermute | solution.py:358
  5.1 0.0 collective-permute-start.8
  5.1 1.5 %fusion = (bf16[64,128]{1,0:T(8,128)(2,1)}, bf16[1,64,128]{2,1,0:T(8,128)(2,1)S(1)}, bf16[1,64,128]{2,1,0:T(8,128)(2,1)}, bf16[1,64,128]{2,1,0:T(8,128)(2,1)}, b...) fusion(bf16[64,16384]{1,0:T(8,128)(2,1)} %bitcast.49), kind=kLoop, calls=%fused_computation.31 | loop fusion | bytes 262144 | tf_op jit(solution)/shard_map/slice | solution.py:328
  6.6 3.6 %collective-permute-start = (bf16[64,128]{1,0:T(8,128)(2,1)}, bf16[64,128]{1,0:T(8,128)(2,1)}, u32[]{:S(2)}, u32[]{:S(2)}) collective-permute-start(bf16[64,128]{1,0:T(8,128)(2,1)} %get-tuple-element.34), channel_id=1, source_target_pairs={{4,0},{8,4},{12,8},{0,12},{5,1},{9,5},{13,9},{1,13},{6,2},{10,6},{... | collective-permute-start | bytes 49160 | tf_op jit(solution)/shard_map/ppermute | solution.py:329
  10.2 0.0 collective-permute-start.1
  10.2 0.5 collective-permute-start.14
  10.6 0.9 %constant_dynamic-update-slice_fusion.2 = bf16[256,768]{1,0:T(8,128)(2,1)S(1)} fusion(bf16[256,256]{1,0:T(8,128)(2,1)} %param.13), kind=kLoop, calls=%fused_computation.28 | loop fusion | bytes 262144
  11.6 0.9 %constant_dynamic-update-slice_fusion.1 = bf16[256,768]{1,0:T(8,128)(2,1)S(1)} fusion(bf16[256,768]{1,0:T(8,128)(2,1)S(1)} %constant_dynamic-update-slice_fusion.2, bf16[256,256]{1,0:T(8,128)(2,1)} %param.14), kind=kLoop, calls=%fused_computation.27 | loop fusion | bytes 262144
  12.5 0.9 %constant_dynamic-update-slice_fusion.refs_7_.refs_10_.refs_14_ = bf16[256,768]{1,0:T(8,128)(2,1)S(1)} fusion(bf16[256,768]{1,0:T(8,128)(2,1)S(1)} %constant_dynamic-update-slice_fusion.1, bf16[256,256]{1,0:T(8,128)(2,1)} %param.15), kind=kLoop, calls=%fused_computation.26 | loop fusion | bytes 262144 | tf_op jit(solution)/shard_map/concatenate | solution.py:364
  13.5 0.0 copy-done
  13.5 0.7 dynamic-slice_bitcast_fusion.9
  14.2 1.0 %dynamic-slice_bitcast_fusion.3 = (bf16[64,1152]{1,0:T(8,128)(2,1)}, bf16[64,1152]{1,0:T(8,128)(2,1)}, bf16[64,1152]{1,0:T(8,128)(2,1)}, bf16[64,1152]{1,0:T(8,1...) fusion(bf16[16384,64]{0,1:T(8,128)(2,1)S(1)} %copy-done, s32[]{:T(128)S(6)} %select_n.105, s32[]{:T(128)S(6)} %select_n.103, ...), kind=kLoop, calls=%fused_computation.3 | loop fusion | bytes 1769496 | tf_op jit(solution)/shard_map/dynamic_slice | solution.py:354
  15.2 0.5 iota_compare_fusion
  16.3 0.0 collective-permute-done
  16.4 1.5 %collective-permute-start.9 = (bf16[64,1280]{1,0:T(8,128)(2,1)}, bf16[64,1280]{1,0:T(8,128)(2,1)S(1)}, u32[]{:S(2)}, u32[]{:S(2)}) collective-permute-start(bf16[64,1280]{1,0:T(8,128)(2,1)} %get-tuple-element.25), channel_id=1, source_target_pairs={{0,2},{1,3},{2,0},{3,1},{4,6},{5,7},{6,4},{7,5},{8,10},{9,11},{10,... | collective-permute-start | bytes 491528 | tf_op jit(solution)/shard_map/ppermute | solution.py:358
  17.8 0.0 collective-permute-done.1
  17.8 0.0 collective-permute-start.11
  17.8 0.8 maximum_select_fusion
  18.7 0.8 pad_maximum_fusion.2
  19.6 0.8 pad_maximum_fusion.1
  20.4 0.8 pad_maximum_fusion
  21.3 0.0 collective-permute-done.10.refs_4_.refs_7_.refs_11_
  21.3 1.1 %collective-permute-start.12 = (bf16[64,1152]{1,0:T(8,128)(2,1)}, bf16[64,1152]{1,0:T(8,128)(2,1)S(1)}, u32[]{:S(2)}, u32[]{:S(2)}) collective-permute-start(bf16[64,1152]{1,0:T(8,128)(2,1)} %get-tuple-element.23), channel_id=1, source_target_pairs={{0,2},{1,3},{2,0},{3,1},{4,6},{5,7},{6,4},{7,5},{8,10},{9,11},{10,... | collective-permute-start | bytes 442376 | tf_op jit(solution)/shard_map/ppermute | solution.py:358
  22.4 0.0 collective-permute-done.8.refs_2_.refs_5_.refs_9_
  22.4 1.0 %collective-permute-start.13 = (bf16[64,1152]{1,0:T(8,128)(2,1)}, bf16[64,1152]{1,0:T(8,128)(2,1)S(1)}, u32[]{:S(2)}, u32[]{:S(2)}) collective-permute-start(bf16[64,1152]{1,0:T(8,128)(2,1)} %get-tuple-element.18), channel_id=1, source_target_pairs={{0,3},{1,0},{2,1},{3,2},{4,7},{5,4},{6,5},{7,6},{8,11},{9,8},{10,9... | collective-permute-start | bytes 442376 | tf_op jit(solution)/shard_map/ppermute | solution.py:358
  23.4 0.3 collective-permute-done.9.refs_3_.refs_6_.refs_10_
  23.7 0.0 collective-permute-start.5
  23.7 0.0 copy-done.1
  23.7 0.0 copy-start.3
  23.7 0.9 %copy-done.3 = bf16[256,256]{1,0:T(8,128)(2,1)S(1)} copy-done((bf16[256,256]{1,0:T(8,128)(2,1)S(1)}, bf16[256,256]{1,0:T(8,128)(2,1)}, u32[]{:S(2)}) %copy-start.3) | copy-done | bytes 131096
  24.6 0.9 %copy-done.4 = bf16[256,256]{1,0:T(8,128)(2,1)S(1)} copy-done((bf16[256,256]{1,0:T(8,128)(2,1)S(1)}, bf16[256,256]{1,0:T(8,128)(2,1)}, u32[]{:S(2)}) %copy-start.4) | copy-done | bytes 131096
  25.5 0.8 copy-done.6
  26.4 0.8 copy-done.7
  27.2 12.7 %layer_chunk_1.1 = (bf16[4096,256]{1,0:T(8,128)(2,1)}, bf16[18,8,512]{2,1,0:T(8,128)(2,1)S(1)}) custom-call(s32[1]{0:T(128)} %bitcast.refs_0_, bf16[64,16384]{1,0:T(8,128)(2,1)S(1)} %bitcast.50, bf16[64,1280]{1,0:T(8,128)(2,1)} %collective-permute-done.8.refs_2_.refs_5_.refs_9_, bf16[64,1280]{1,0:T(8,128)(2,1)S(1)} %collective-permute-done.9.refs_3_.refs_6_.refs_10_, ...), custom_call_target="tpu_custom_call" | custom-call | flops 3925868544 | bytes 5373952 | tf_op jit(solution)/shard_map/layer_chunk_1/pallas_call | solution.py:255
  39.9 0.0 collective-permute-done.11.refs_2_.refs_5_
  40.0 1.5 %collective-permute-start.6 = (bf16[64,1152]{1,0:T(8,128)(2,1)S(1)}, bf16[64,1152]{1,0:T(8,128)(2,1)S(1)}, u32[]{:S(2)}, u32[]{:S(2)}) collective-permute-start(bf16[64,1152]{1,0:T(8,128)(2,1)S(1)} %copy-done.9), channel_id=1, source_target_pairs={{0,2},{1,3},{2,0},{3,1},{4,6},{5,7},{6,4},{7,5},{8,10},{9,11},{10,... | collective-permute-start | bytes 442376 | tf_op jit(solution)/shard_map/ppermute | solution.py:358
  41.4 0.0 collective-permute-done.12.refs_3_.refs_6_
  41.4 1.5 %collective-permute-start.7 = (bf16[64,1152]{1,0:T(8,128)(2,1)S(1)}, bf16[64,1152]{1,0:T(8,128)(2,1)S(1)}, u32[]{:S(2)}, u32[]{:S(2)}) collective-permute-start(bf16[64,1152]{1,0:T(8,128)(2,1)S(1)} %copy-done.8), channel_id=1, source_target_pairs={{0,3},{1,0},{2,1},{3,2},{4,7},{5,4},{6,5},{7,6},{8,11},{9,8},{10,9... | collective-permute-start | bytes 442376 | tf_op jit(solution)/shard_map/ppermute | solution.py:358
  42.9 0.0 collective-permute-done.13.refs_4_.refs_7_
  42.9 0.1 collective-permute-start.4
  43.0 12.4 %layer_chunk_10.1 = (bf16[4096,256]{1,0:T(8,128)(2,1)}, bf16[18,8,512]{2,1,0:T(8,128)(2,1)S(1)}) custom-call(s32[1]{0:T(128)} %bitcast.refs_0_, bf16[64,16384]{1,0:T(8,128)(2,1)S(1)} %bitcast.51, bf16[64,1152]{1,0:T(8,128)(2,1)S(1)} %collective-permute-done.11.refs_2_.refs_5_, ...), custom_call_target="tpu_custom_call", output_to_operand_aliasing={{0}: (16, {})} | custom-call | flops 3925868544 | bytes 5373952 | tf_op jit(solution)/shard_map/layer_chunk_10/pallas_call | solution.py:255
  55.4 0.0 collective-permute-done.5.refs_2_.refs_5_
  55.4 0.7 collective-permute-start.3
  56.1 0.0 collective-permute-done.6.refs_3_.refs_6_
  56.1 0.2 collective-permute-start.2
  56.2 0.0 collective-permute-done.7.refs_4_.refs_7_
  56.3 12.4 %layer_chunk_19.1 = (bf16[4096,256]{1,0:T(8,128)(2,1)}, bf16[18,8,512]{2,1,0:T(8,128)(2,1)S(1)}) custom-call(s32[1]{0:T(128)} %bitcast.refs_0_, bf16[64,16384]{1,0:T(8,128)(2,1)S(1)} %bitcast.52, bf16[64,1152]{1,0:T(8,128)(2,1)S(1)} %collective-permute-done.5.refs_2_.refs_5_, ...), custom_call_target="tpu_custom_call", output_to_operand_aliasing={{0}: (16, {})} | custom-call | flops 3925868544 | bytes 5373952 | tf_op jit(solution)/shard_map/layer_chunk_19/pallas_call | solution.py:255
  68.7 1.4 %collective-permute-start.17 = (bf16[18,8,512]{2,1,0:T(8,128)(2,1)S(1)}, bf16[18,8,512]{2,1,0:T(8,128)(2,1)S(1)}, u32[]{:S(2)}, u32[]{:S(2)}) collective-permute-start(bf16[18,8,512]{2,1,0:T(8,128)(2,1)S(1)} %get-tuple-element.16.refs_2_), channel_id=1, source_target_pairs={{0,1},{1,2},{2,3},{3,4},{4,5},{5,6},{6,7},{7,8},{8,9},{9,10},{10,1... | collective-permute-start | bytes 442376 | tf_op jit(solution)/shard_map/ppermute | solution.py:394
  70.1 0.0 collective-permute-done.4.refs_4_
  70.1 0.2 collective-permute-start.16
  70.2 0.0 collective-permute-done.3.refs_3_
  70.2 0.6 collective-permute-start.15
  70.8 0.0 collective-permute-done.2.refs_2_
  70.8 8.8 %layer_chunk_28.1 = (bf16[4096,256]{1,0:T(8,128)(2,1)}, bf16[12,8,512]{2,1,0:T(8,128)(2,1)S(1)}) custom-call(s32[1]{0:T(128)} %bitcast.refs_0_, bf16[64,16384]{1,0:T(8,128)(2,1)S(1)} %bitcast.53, bf16[64,640]{1,0:T(8,128)(2,1)S(1)} %collective-permute-done.2.refs_2_, ...), custom_call_target="tpu_custom_call", output_to_operand_aliasing={{0}: (20, {})} | custom-call | flops 2617245696 | bytes 4980736 | tf_op jit(solution)/shard_map/layer_chunk_28/pallas_call | solution.py:255
  79.6 0.3 collective-permute-start.18
  79.9 0.0 collective-permute-done.14
  79.9 0.6 pad_add_fusion.counts
  80.5 5.9 %collective-permute-done.18.refs_7_ = bf16[12,8,512]{2,1,0:T(8,128)(2,1)S(1)} collective-permute-done((bf16[12,8,512]{2,1,0:T(8,128)(2,1)S(1)}, bf16[12,8,512]{2,1,0:T(8,128)(2,1)S(1)}, u32[]{:S(2)}, u32[]{:S(2)}) %collective-permute-start.18) | collective-permute-done | bytes 98336 | tf_op jit(solution)/shard_map/ppermute | solution.py:394
  86.4 0.0 collective-permute-done.17.refs_6_
  86.4 0.0 collective-permute-done.16.refs_5_
  86.4 0.0 collective-permute-done.15.refs_4_
  86.4 2.3 %place_tiles.1 = bf16[128,8,512]{2,1,0:T(8,128)(2,1)} custom-call(s32[2]{0:T(128)S(1)} %pad_add_fusion.counts, bf16[18,8,512]{2,1,0:T(8,128)(2,1)S(1)} %get-tuple-element.14.refs_0_, bf16[18,8,512]{2,1,0:T(8,128)(2,1)S(1)} %get-tuple-element.15.refs_1_, bf16[18,8,512]{2,1,0:T(8,128)(2,1)S(1)} %get-tuple-element.16.refs_2_, ...), custom_call_target="tpu_custom_call" | custom-call | tf_op jit(solution)/shard_map/place_tiles/pallas_call | solution.py:400
  (13 shorter events, 0.0 us)
Async XLA Ops:
  0.6 12.9 %copy-start = (bf16[16384,64]{0,1:T(8,128)(2,1)S(1)}, bf16[16384,64]{0,1:T(8,128)(2,1)}, u32[]{:S(2)}) copy-start(bf16[16384,64]{0,1:T(8,128)(2,1)} %param.12) | copy-start | bytes 6291460
  2.7 21.0 %copy-start.1 = (bf16[256,1024]{1,0:T(8,128)(2,1)S(1)}, bf16[256,1024]{1,0:T(8,128)(2,1)}, u32[]{:S(2)}) copy-start(bf16[256,1024]{1,0:T(8,128)(2,1)} %refs_16_.1) | copy-start | bytes 1572868
  2.7 21.0 %copy-start.2 = (bf16[1024,256]{1,0:T(8,128)(2,1)S(1)}, bf16[1024,256]{1,0:T(8,128)(2,1)}, u32[]{:S(2)}) copy-start(bf16[1024,256]{1,0:T(8,128)(2,1)} %refs_17_.1) | copy-start | bytes 1572868
  2.7 18.6 %collective-permute-start.10 = (bf16[64,1280]{1,0:T(8,128)(2,1)}, bf16[64,1280]{1,0:T(8,128)(2,1)}, u32[]{:S(2)}, u32[]{:S(2)}) collective-permute-start(bf16[64,1280]{1,0:T(8,128)(2,1)} %get-tuple-element.24), channel_id=1, source_target_pairs={{0,3},{1,0},{2,1},{3,2},{4,7},{5,4},{6,5},{7,6},{8,11},{9,8},{10,9... | collective-permute-start | bytes 491528 | tf_op jit(solution)/shard_map/ppermute | solution.py:358
  5.1 17.3 %collective-permute-start.8 = (bf16[64,1280]{1,0:T(8,128)(2,1)}, bf16[64,1280]{1,0:T(8,128)(2,1)}, u32[]{:S(2)}, u32[]{:S(2)}) collective-permute-start(bf16[64,1280]{1,0:T(8,128)(2,1)} %get-tuple-element.26), channel_id=1, source_target_pairs={{0,1},{1,2},{2,3},{3,0},{4,5},{5,6},{6,7},{7,4},{8,9},{9,10},{10,1... | collective-permute-start | bytes 491528 | tf_op jit(solution)/shard_map/ppermute | solution.py:358
  6.6 9.8 %collective-permute-start = (bf16[64,128]{1,0:T(8,128)(2,1)}, bf16[64,128]{1,0:T(8,128)(2,1)}, u32[]{:S(2)}, u32[]{:S(2)}) collective-permute-start(bf16[64,128]{1,0:T(8,128)(2,1)} %get-tuple-element.34), channel_id=1, source_target_pairs={{4,0},{8,4},{12,8},{0,12},{5,1},{9,5},{13,9},{1,13},{6,2},{10,6},{... | collective-permute-start | bytes 49160 | tf_op jit(solution)/shard_map/ppermute | solution.py:329
  10.2 7.6 %collective-permute-start.1 = (bf16[64,128]{1,0:T(8,128)(2,1)}, bf16[64,128]{1,0:T(8,128)(2,1)}, u32[]{:S(2)}, u32[]{:S(2)}) collective-permute-start(bf16[64,128]{1,0:T(8,128)(2,1)} %get-tuple-element.30), channel_id=1, source_target_pairs={{0,4},{4,8},{8,12},{12,0},{1,5},{5,9},{9,13},{13,1},{2,6},{6,10},{... | collective-permute-start | bytes 49160 | tf_op jit(solution)/shard_map/ppermute | solution.py:330
  10.2 69.7 %collective-permute-start.14 = (s32[1]{0:T(128)}, s32[1]{0:T(128)}, u32[]{:S(2)}, u32[]{:S(2)}) collective-permute-start(s32[1]{0:T(128)} %param.20), channel_id=1, source_target_pairs={{0,1},{1,2},{2,3},{3,4},{4,5},{5,6},{6,7},{7,8},{8,9},{9,10},{10,1... | collective-permute-start | bytes 20 | tf_op jit(solution)/shard_map/ppermute | solution.py:372
  16.4 7.3 %collective-permute-start.9 = (bf16[64,1280]{1,0:T(8,128)(2,1)}, bf16[64,1280]{1,0:T(8,128)(2,1)S(1)}, u32[]{:S(2)}, u32[]{:S(2)}) collective-permute-start(bf16[64,1280]{1,0:T(8,128)(2,1)} %get-tuple-element.25), channel_id=1, source_target_pairs={{0,2},{1,3},{2,0},{3,1},{4,6},{5,7},{6,4},{7,5},{8,10},{9,11},{10,... | collective-permute-start | bytes 491528 | tf_op jit(solution)/shard_map/ppermute | solution.py:358
  17.8 22.1 %collective-permute-start.11 = (bf16[64,1152]{1,0:T(8,128)(2,1)}, bf16[64,1152]{1,0:T(8,128)(2,1)S(1)}, u32[]{:S(2)}, u32[]{:S(2)}) collective-permute-start(bf16[64,1152]{1,0:T(8,128)(2,1)} %get-tuple-element.19), channel_id=1, source_target_pairs={{0,1},{1,2},{2,3},{3,0},{4,5},{5,6},{6,7},{7,4},{8,9},{9,10},{10,1... | collective-permute-start | bytes 442376 | tf_op jit(solution)/shard_map/ppermute | solution.py:358
  21.3 20.2 %collective-permute-start.12 = (bf16[64,1152]{1,0:T(8,128)(2,1)}, bf16[64,1152]{1,0:T(8,128)(2,1)S(1)}, u32[]{:S(2)}, u32[]{:S(2)}) collective-permute-start(bf16[64,1152]{1,0:T(8,128)(2,1)} %get-tuple-element.23), channel_id=1, source_target_pairs={{0,2},{1,3},{2,0},{3,1},{4,6},{5,7},{6,4},{7,5},{8,10},{9,11},{10,... | collective-permute-start | bytes 442376 | tf_op jit(solution)/shard_map/ppermute | solution.py:358
  22.4 20.5 %collective-permute-start.13 = (bf16[64,1152]{1,0:T(8,128)(2,1)}, bf16[64,1152]{1,0:T(8,128)(2,1)S(1)}, u32[]{:S(2)}, u32[]{:S(2)}) collective-permute-start(bf16[64,1152]{1,0:T(8,128)(2,1)} %get-tuple-element.18), channel_id=1, source_target_pairs={{0,3},{1,0},{2,1},{3,2},{4,7},{5,4},{6,5},{7,6},{8,11},{9,8},{10,9... | collective-permute-start | bytes 442376 | tf_op jit(solution)/shard_map/ppermute | solution.py:358
  23.7 31.7 %collective-permute-start.5 = (bf16[64,1152]{1,0:T(8,128)(2,1)}, bf16[64,1152]{1,0:T(8,128)(2,1)S(1)}, u32[]{:S(2)}, u32[]{:S(2)}) collective-permute-start(bf16[64,1152]{1,0:T(8,128)(2,1)} %get-tuple-element.22), channel_id=1, source_target_pairs={{0,1},{1,2},{2,3},{3,0},{4,5},{5,6},{6,7},{7,4},{8,9},{9,10},{10,1... | collective-permute-start | bytes 442376 | tf_op jit(solution)/shard_map/ppermute | solution.py:358
  23.7 0.9 %copy-start.3 = (bf16[256,256]{1,0:T(8,128)(2,1)S(1)}, bf16[256,256]{1,0:T(8,128)(2,1)}, u32[]{:S(2)}) copy-start(bf16[256,256]{1,0:T(8,128)(2,1)} %refs_15_.5) | copy-start | bytes 393220
  24.6 0.9 %copy-start.4 = (bf16[256,256]{1,0:T(8,128)(2,1)S(1)}, bf16[256,256]{1,0:T(8,128)(2,1)}, u32[]{:S(2)}) copy-start(bf16[256,256]{1,0:T(8,128)(2,1)} %constant.90.clone.refs_6_.refs_9_.refs_13_) | copy-start | bytes 393220
  25.5 0.8 copy-start.6
  26.4 0.8 copy-start.7
  27.2 12.7 %copy-start.9 = (bf16[64,1152]{1,0:T(8,128)(2,1)S(1)}, bf16[64,1152]{1,0:T(8,128)(2,1)}, u32[]{:S(2)}) copy-start(bf16[64,1152]{1,0:T(8,128)(2,1)} %get-tuple-element.21) | copy-start | bytes 442372
  27.2 14.2 %copy-start.8 = (bf16[64,1152]{1,0:T(8,128)(2,1)S(1)}, bf16[64,1152]{1,0:T(8,128)(2,1)}, u32[]{:S(2)}) copy-start(bf16[64,1152]{1,0:T(8,128)(2,1)} %get-tuple-element.20) | copy-start | bytes 442372
  27.2 15.7 %copy-start.5 = (bf16[256,256]{1,0:T(8,128)(2,1)S(1)}, bf16[256,256]{1,0:T(8,128)(2,1)}, u32[]{:S(2)}) copy-start(bf16[256,256]{1,0:T(8,128)(2,1)} %constant.90.clone.refs_6_.refs_9_.refs_13_) | copy-start | bytes 393220
  40.0 16.1 %collective-permute-start.6 = (bf16[64,1152]{1,0:T(8,128)(2,1)S(1)}, bf16[64,1152]{1,0:T(8,128)(2,1)S(1)}, u32[]{:S(2)}, u32[]{:S(2)}) collective-permute-start(bf16[64,1152]{1,0:T(8,128)(2,1)S(1)} %copy-done.9), channel_id=1, source_target_pairs={{0,2},{1,3},{2,0},{3,1},{4,6},{5,7},{6,4},{7,5},{8,10},{9,11},{10,... | collective-permute-start | bytes 442376 | tf_op jit(solution)/shard_map/ppermute | solution.py:358
  41.4 14.8 %collective-permute-start.7 = (bf16[64,1152]{1,0:T(8,128)(2,1)S(1)}, bf16[64,1152]{1,0:T(8,128)(2,1)S(1)}, u32[]{:S(2)}, u32[]{:S(2)}) collective-permute-start(bf16[64,1152]{1,0:T(8,128)(2,1)S(1)} %copy-done.8), channel_id=1, source_target_pairs={{0,3},{1,0},{2,1},{3,2},{4,7},{5,4},{6,5},{7,6},{8,11},{9,8},{10,9... | collective-permute-start | bytes 442376 | tf_op jit(solution)/shard_map/ppermute | solution.py:358
  42.9 27.2 %collective-permute-start.4 = (bf16[64,640]{1,0:T(8,128)(2,1)S(1)}, bf16[64,640]{1,0:T(8,128)(2,1)S(1)}, u32[]{:S(2)}, u32[]{:S(2)}) collective-permute-start(bf16[64,640]{1,0:T(8,128)(2,1)S(1)} %pad_maximum_fusion.2), channel_id=1, source_target_pairs={{0,3},{1,0},{2,1},{3,2},{4,7},{5,4},{6,5},{7,6},{8,11},{9,8},{10,9... | collective-permute-start | bytes 245768 | tf_op jit(solution)/shard_map/ppermute | solution.py:358
  55.4 14.8 %collective-permute-start.3 = (bf16[64,640]{1,0:T(8,128)(2,1)S(1)}, bf16[64,640]{1,0:T(8,128)(2,1)S(1)}, u32[]{:S(2)}, u32[]{:S(2)}) collective-permute-start(bf16[64,640]{1,0:T(8,128)(2,1)S(1)} %pad_maximum_fusion.1), channel_id=1, source_target_pairs={{0,2},{1,3},{2,0},{3,1},{4,6},{5,7},{6,4},{7,5},{8,10},{9,11},{10,... | collective-permute-start | bytes 245768 | tf_op jit(solution)/shard_map/ppermute | solution.py:358
  56.1 14.7 %collective-permute-start.2 = (bf16[64,640]{1,0:T(8,128)(2,1)S(1)}, bf16[64,640]{1,0:T(8,128)(2,1)S(1)}, u32[]{:S(2)}, u32[]{:S(2)}) collective-permute-start(bf16[64,640]{1,0:T(8,128)(2,1)S(1)} %pad_maximum_fusion), channel_id=1, source_target_pairs={{0,1},{1,2},{2,3},{3,0},{4,5},{5,6},{6,7},{7,4},{8,9},{9,10},{10,1... | collective-permute-start | bytes 245768 | tf_op jit(solution)/shard_map/ppermute | solution.py:358
  68.7 17.7 %collective-permute-start.17 = (bf16[18,8,512]{2,1,0:T(8,128)(2,1)S(1)}, bf16[18,8,512]{2,1,0:T(8,128)(2,1)S(1)}, u32[]{:S(2)}, u32[]{:S(2)}) collective-permute-start(bf16[18,8,512]{2,1,0:T(8,128)(2,1)S(1)} %get-tuple-element.16.refs_2_), channel_id=1, source_target_pairs={{0,1},{1,2},{2,3},{3,4},{4,5},{5,6},{6,7},{7,8},{8,9},{9,10},{10,1... | collective-permute-start | bytes 442376 | tf_op jit(solution)/shard_map/ppermute | solution.py:394
  70.1 16.3 %collective-permute-start.16 = (bf16[18,8,512]{2,1,0:T(8,128)(2,1)S(1)}, bf16[18,8,512]{2,1,0:T(8,128)(2,1)S(1)}, u32[]{:S(2)}, u32[]{:S(2)}) collective-permute-start(bf16[18,8,512]{2,1,0:T(8,128)(2,1)S(1)} %get-tuple-element.15.refs_1_), channel_id=1, source_target_pairs={{0,1},{1,2},{2,3},{3,4},{4,5},{5,6},{6,7},{7,8},{8,9},{9,10},{10,1... | collective-permute-start | bytes 442376 | tf_op jit(solution)/shard_map/ppermute | solution.py:394
  70.2 16.2 %collective-permute-start.15 = (bf16[18,8,512]{2,1,0:T(8,128)(2,1)S(1)}, bf16[18,8,512]{2,1,0:T(8,128)(2,1)S(1)}, u32[]{:S(2)}, u32[]{:S(2)}) collective-permute-start(bf16[18,8,512]{2,1,0:T(8,128)(2,1)S(1)} %get-tuple-element.14.refs_0_), channel_id=1, source_target_pairs={{0,1},{1,2},{2,3},{3,4},{4,5},{5,6},{6,7},{7,8},{8,9},{9,10},{10,1... | collective-permute-start | bytes 442376 | tf_op jit(solution)/shard_map/ppermute | solution.py:394
  79.6 6.8 %collective-permute-start.18 = (bf16[12,8,512]{2,1,0:T(8,128)(2,1)S(1)}, bf16[12,8,512]{2,1,0:T(8,128)(2,1)S(1)}, u32[]{:S(2)}, u32[]{:S(2)}) collective-permute-start(bf16[12,8,512]{2,1,0:T(8,128)(2,1)S(1)} %get-tuple-element.17.refs_3_), channel_id=1, source_target_pairs={{0,1},{1,2},{2,3},{3,4},{4,5},{5,6},{6,7},{7,8},{8,9},{9,10},{10,1... | collective-permute-start | bytes 294920 | tf_op jit(solution)/shard_map/ppermute | solution.py:394
where the time goes:
time: 89.3 us; the launch traced here: 88.7 us
  Pallas kernels  48.6 us (54%)
  starting transfers between devices  16.3 us (18%)
  local copies, waits for them, and re-layouts  11.4 us (13%)
  waiting for transfers between devices  6.21 us (7%)
  other arithmetic  4.54 us (5%)
  between operations  1.59 us (2%)
    pallas_call x4, Pallas kernels, run_chunk(): pl.pallas_call(functools.partial(chunk_kernel, spec), out_shape=(jax.Shap...  46.3 us
    ppermute x12, starting transfers between devices, body(): lax.ppermute(block, 'mp', [(i, (i + s) % ways) for i in range(ways)])  9.85 us
    ppermute x4, waiting for transfers between devices, body(): came_pooled.append(lax.ppermute(pooled, ('seq', 'mp'), pairs))  5.87 us
    unnamed x22, local copies, waits for them, and re-layouts  5.33 us
    dynamic_slice x3, local copies, waits for them, and re-layouts, body(): lax.dynamic_slice_in_dim(own, dest * quarter + tile * BLOCK, count * BLOC...  3.66 us
    ppermute x1, starting transfers between devices, body(): lax.ppermute(first, 'seq', [((i + 1) % seq_ways, i) for i in range(seq_wa...  3.6 us
    concatenate x3, other arithmetic, body(): block = jnp.concatenate([block, halo], axis=1)  2.54 us
    ppermute x4, starting transfers between devices, body(): came_pooled.append(lax.ppermute(pooled, ('seq', 'mp'), pairs))  2.44 us
  transfers between devices with their start and end apart: 19, of which 2 were waited for; matrix products, arithmetic and copies ran while one was open for 12% of the time, Pallas kernels for 52%

commit v1 on v0

v1 whole, which is shorter than its diff:
```python
import functools
import math

import jax
import jax.numpy as jnp
from jax import lax
from jax.experimental import pallas as pl
from jax.experimental.pallas import tpu as pltpu
from jax.sharding import PartitionSpec as P

HEADS = 8
WINDOW = 32
DILATION = 4
TILE_PARENTS = 16
CHILDREN = 8
BLOCK = WINDOW * DILATION
HALF = BLOCK // 2
CHUNKS = (7, 13, 13)
FFN_ROWS = 384
FFN_COLS = 256
SHIFTS = (3, 2, 1)

BF = jnp.bfloat16
F32 = jnp.float32


def gather_order():
    row = lax.broadcasted_iota(jnp.int32, (BLOCK, 2 * BLOCK), 0)
    col = lax.broadcasted_iota(jnp.int32, (BLOCK, 2 * BLOCK), 1)
    return (col == HALF + DILATION * (row % WINDOW) + row // WINDOW).astype(F32).astype(BF)


def output_order():
    row = lax.broadcasted_iota(jnp.int32, (2 * BLOCK, BLOCK), 0)
    col = lax.broadcasted_iota(jnp.int32, (2 * BLOCK, BLOCK), 1)
    point = DILATION * (col % WINDOW) + col // WINDOW
    by_child = BLOCK + (point % CHILDREN) * TILE_PARENTS + point // CHILDREN
    return ((row == point) | (row == by_child)).astype(F32).astype(BF)


def head_mask(width):
    rows = HEADS * WINDOW
    row = lax.broadcasted_iota(jnp.int32, (rows, width), 0)
    col = lax.broadcasted_iota(jnp.int32, (rows, width), 1)
    return (row // (WINDOW // 2) % HEADS == col // (width // HEADS)).astype(F32).astype(BF)


def norm_rows(values):
    centre = values - jnp.mean(values, axis=-1, keepdims=True)
    spread = jnp.mean(centre * centre, axis=-1, keepdims=True)
    return centre * lax.rsqrt(spread + 1e-05)


def dot_nn(a, b):
    return lax.dot_general(a, b, (((1,), (0,)), ((), ())), preferred_element_type=F32)


def dot_nt(a, b):
    return lax.dot_general(a, b, (((1,), (1,)), ((), ())), preferred_element_type=F32)


def segment_max(scores):
    width = scores.shape[1] // 2
    run = WINDOW // 2
    top = jnp.maximum(scores[:, :width], scores[:, width:])
    for shift in (1, 2, 4, 8):
        top = jnp.maximum(top, pltpu.roll(top, shift, 1))
    lane = lax.broadcasted_iota(jnp.int32, top.shape, 1)
    top = jnp.where(lane % run == run - 1, top, -jnp.inf)
    for shift in (1, 2, 4, 8):
        top = jnp.maximum(top, pltpu.roll(top, width - shift, 1))
    return top


def feed_forward(hidden, normed, up_ref, down_ref):
    hidden_width = up_ref.shape[1]
    rows = hidden.shape[0]
    done = []
    for r in range(0, rows, FFN_ROWS):
        part = slice(r, min(r + FFN_ROWS, rows))
        total = hidden[part]
        for c in range(0, hidden_width, FFN_COLS):
            up = dot_nn(normed[part], up_ref[:, c : c + FFN_COLS])
            inner = up * (0.7978845608028654 + 0.035677408136300125 * (up * up))
            half = 0.5 * up
            activated = (half + half * jnp.tanh(inner)).astype(BF)
            total = total + dot_nn(activated, down_ref[c : c + FFN_COLS, :])
        done.append(total.astype(BF))
    return jnp.concatenate(done, axis=0)


def layer(x, weights, arrive, windows):
    wq, wk, wv, wo, wu, wd = weights
    width = x.shape[1]
    normed = norm_rows(x).astype(BF)
    arrive(0, 3)
    queries = dot_nn(normed, wq[...]).astype(BF)
    keys = dot_nn(normed, wk[...]).astype(BF)
    values = dot_nn(normed, wv[...]).astype(BF)
    mask = head_mask(width)
    run = WINDOW // 2
    groups = windows * DILATION
    scores = []
    for g in range(groups):
        rows = slice(g * WINDOW, (g + 1) * WINDOW)
        k = keys[rows]
        wide = jnp.concatenate([k[:run]] * HEADS + [k[run:]] * HEADS, axis=0) * mask
        scores.append(dot_nt(queries[rows], wide))
    scores = jnp.concatenate(scores, axis=0)
    top = segment_max(scores)
    top = jnp.concatenate([top, top], axis=1)
    factor = math.log2(math.e) / math.sqrt(width // HEADS)
    shares = jnp.exp2((scores - top) * factor).astype(BF)
    total = dot_nn(shares, mask)
    mixed = []
    for g in range(groups):
        rows = slice(g * WINDOW, (g + 1) * WINDOW)
        v = values[rows]
        wide = jnp.concatenate([v[:run]] * HEADS + [v[run:]] * HEADS, axis=0) * mask
        mixed.append(dot_nn(shares[rows], wide))
    attended = (jnp.concatenate(mixed, axis=0) / total).astype(BF)
    arrive(3, 6)
    hidden = x + dot_nn(attended, wo[...])
    return feed_forward(hidden, norm_rows(hidden).astype(BF), wu, wd)


def send_kernel(quarter, wanted, mp_ref, own, *refs):
    count = len(wanted)
    outs, bufs, sems = refs[:count], refs[count : 2 * count], refs[2 * count]
    loads, puts = [], []
    for n, (shift, tile, tiles) in enumerate(wanted):
        col = tile * BLOCK
        if shift is not None:
            col = pl.multiple_of((mp_ref[0] ^ shift) * quarter + col, BLOCK)
        loads.append(pltpu.make_async_copy(own.at[:, pl.ds(col, tiles * BLOCK)], bufs[n], sems.at[0, n]))
        puts.append(pltpu.make_async_copy(bufs[n], outs[n], sems.at[1, n]))
    for c in loads:
        c.start()
    for load, put in zip(loads, puts):
        load.wait()
        put.start()
    for c in puts:
        c.wait()


def send_blocks(mp_index, own, quarter, wanted, name):
    hbm = pl.BlockSpec(memory_space=pltpu.HBM)
    return pl.pallas_call(
        functools.partial(send_kernel, quarter, wanted),
        out_shape=tuple(jax.ShapeDtypeStruct((own.shape[0], t * BLOCK), BF) for _, _, t in wanted),
        in_specs=[pl.BlockSpec(memory_space=pltpu.SMEM), hbm],
        out_specs=(hbm,) * len(wanted),
        scratch_shapes=[pltpu.VMEM((own.shape[0], t * BLOCK), BF) for _, _, t in wanted]
        + [pltpu.SemaphoreType.DMA((2, len(wanted)))],
        name=name,
    )(mp_index, *in_hbm([own]))


def last_blocks(spec, mp_index, own, after, prior, outs, bufs, edge, halo, edge_sems, load_sems, put_sems):
    quarter, ways, tile, tiles = spec
    edges, loads = [], []
    for q in range(ways):
        head = own.at[:, pl.ds((q + 1) * quarter, BLOCK)] if q + 1 < ways else after
        tail = own.at[:, pl.ds(q * quarter - BLOCK, BLOCK)] if q else prior
        edges.append(pltpu.make_async_copy(head, edge.at[0, q], edge_sems.at[2 * q]))
        edges.append(pltpu.make_async_copy(tail, edge.at[1, q], edge_sems.at[2 * q + 1]))
    for n in range(ways - 1):
        col = pl.multiple_of((mp_index ^ SHIFTS[n]) * quarter + tile * BLOCK, BLOCK)
        dst = bufs[n].at[:, pl.ds(0, tiles * BLOCK)]
        loads.append(pltpu.make_async_copy(own.at[:, pl.ds(col, tiles * BLOCK)], dst, load_sems.at[n]))
    puts = [pltpu.make_async_copy(bufs[n], outs[n], put_sems.at[n]) for n in range(ways - 1)]
    puts.append(pltpu.make_async_copy(halo.at[mp_index], outs[ways - 1], put_sems.at[ways - 1]))

    def begin():
        for c in edges + loads:
            c.start()

    def send():
        for c in edges + loads:
            c.wait()
        lane = lax.broadcasted_iota(jnp.int32, edge.shape[1:], 2)
        halo[...] = jnp.where(lane < HALF, edge[0].astype(F32), edge[1].astype(F32)).astype(BF)
        for n in range(ways - 1):
            bufs[n][:, tiles * BLOCK :] = halo[mp_index ^ SHIFTS[n]]
        for c in puts:
            c.start()

    def end():
        for c in puts:
            c.wait()

    return begin, send, end


def chunk_kernel(spec, *refs):
    first_tile, tiles, first_window, windows, last, aliased, quarter, feat, last_span = spec
    n_recv = 3
    it = iter(refs)
    place_ref = next(it)
    kept_ref = next(it)
    own = next(it)
    recv = [next(it) for _ in range(n_recv)]
    if first_window > 1:
        before = [next(it) for _ in range(n_recv)]
    if last:
        halo_own = next(it)
        start = [next(it) for _ in range(n_recv)]
        next(it)
    if not aliased:
        after, prior = next(it), next(it)
    weights_hbm = [next(it) for _ in range(7)]
    if aliased:
        next(it)
    refined, pooled = next(it), next(it)
    if not aliased:
        block_outs = [next(it) for _ in range(n_recv + 1)]
    xbuf, ybuf, pbuf, pooled_buf = (next(it) for _ in range(4))
    weights = [next(it) for _ in range(7)]
    in_sem, w_sem, out_sem, pool_sem = (next(it) for _ in range(4))
    mp_index = place_ref[0]
    if not aliased:
        block_bufs = [next(it) for _ in range(n_recv)]
        begin, send, end = last_blocks(
            (quarter, n_recv + 1) + last_span, mp_index, own, after, prior, block_outs, block_bufs, *it
        )
    copies = []
    fetch = [pltpu.make_async_copy(weights_hbm[n], weights[n], w_sem.at[n]) for n in range(7)]

    def arrive(first, limit):
        for n in range(first, limit):
            fetch[n].wait()

    def bring(src, shift, col, width):
        j = mp_index ^ shift
        dst = xbuf.at[pl.ds(pl.multiple_of(j * feat, feat), feat), pl.ds(col, width)]
        c = pltpu.make_async_copy(src, dst, in_sem.at[len(copies)])
        c.start()
        copies.append(c)

    def own_cols(tile, count):
        return own.at[:, pl.ds(pl.multiple_of(mp_index * quarter + tile * BLOCK, BLOCK), count * BLOCK)]

    lead = 0
    if first_window > 1:
        lead = 1
        for s in range(n_recv):
            n_before = before[s].shape[1]
            bring(before[s].at[:, pl.ds(n_before - BLOCK, BLOCK)], n_recv - s, 0, BLOCK)
        bring(own_cols(first_tile - 1, 1), 0, 0, BLOCK)
    for s in range(n_recv):
        bring(recv[s], n_recv - s, lead * BLOCK, recv[s].shape[1])
    bring(own_cols(first_tile, tiles), 0, lead * BLOCK, tiles * BLOCK)
    if last:
        bring(halo_own, 0, (lead + tiles) * BLOCK, BLOCK)
        for s in range(n_recv):
            bring(start[s].at[:, pl.ds(0, BLOCK)], n_recv - s, (lead + tiles + 1) * BLOCK, BLOCK)
        bring(own_cols(0, 1), 0, (lead + tiles + 1) * BLOCK, BLOCK)
    for n in range(3):
        fetch[n].start()
    gather = gather_order()
    back = output_order()
    for c in copies:
        c.wait()
    for n in range(3, 7):
        fetch[n].start()
    if not aliased:
        begin()

    width = 4 * feat
    xs = [dot_nt(gather, xbuf[:, n * BLOCK : (n + 2) * BLOCK]) for n in range(windows)]
    ys = layer(jnp.concatenate(xs, axis=0), weights[:6], arrive, windows)
    for n in range(windows):
        both = dot_nn(back, ys[n * BLOCK : (n + 1) * BLOCK]).astype(BF)
        ybuf[n * BLOCK : (n + 1) * BLOCK, :] = both[:BLOCK]
        for c in range(CHILDREN):
            piece = both[BLOCK + c * TILE_PARENTS : BLOCK + (c + 1) * TILE_PARENTS]
            pbuf[n * TILE_PARENTS : (n + 1) * TILE_PARENTS, c * width : (c + 1) * width] = piece
    if not aliased:
        send()
    base = first_window * BLOCK - HALF
    outs = []
    if last:
        rows = quarter - base
        outs.append(pltpu.make_async_copy(ybuf.at[pl.ds(0, rows)], refined.at[pl.ds(base, rows)], out_sem.at[0]))
        outs.append(
            pltpu.make_async_copy(
                ybuf.at[pl.ds(windows * BLOCK - HALF, HALF)], refined.at[pl.ds(0, HALF)], out_sem.at[1]
            )
        )
    else:
        rows = windows * BLOCK
        outs.append(pltpu.make_async_copy(ybuf, refined.at[pl.ds(base, rows)], out_sem.at[0]))
    for c in outs:
        c.start()
    arrive(6, 7)
    result = dot_nn(pbuf[...], weights[6][...])
    halves = windows * TILE_PARENTS // 8
    pooled_buf[:halves] = result.reshape((halves,) + pooled_buf.shape[1:]).astype(BF)
    if not aliased:
        pooled_buf[halves] = jnp.full(pooled_buf.shape[1:], kept_ref[0], jnp.int32).astype(F32).astype(BF)
    c = pltpu.make_async_copy(pooled_buf, pooled, pool_sem.at[0])
    c.start()
    c.wait()
    for c in outs:
        c.wait()
    if not aliased:
        end()


def run_chunk(spec, mp_index, kept, own, recv, before, halo_own, start, tied, edges, weights, refined, rows):
    first_tile, tiles, first_window, windows, last, aliased, quarter, feat, last_span = spec
    width = 4 * feat
    pool_width = weights[6].shape[1]
    smem = pl.BlockSpec(memory_space=pltpu.SMEM)
    hbm = pl.BlockSpec(memory_space=pltpu.HBM)
    any_spec = pl.BlockSpec(memory_space=pl.ANY)
    args = [mp_index, kept] + in_hbm([own]) + recv
    if first_window > 1:
        args += before
    if last:
        args += [halo_own] + start + [tied]
    if not aliased:
        args += edges
    moved = len(args)
    args += weights
    aliases = {}
    if aliased:
        aliases = {len(args): 0}
        args.append(refined)
    halves = windows * TILE_PARENTS // 8
    points = windows * BLOCK
    flops = 2 * points * (width * width * 16 + 2 * width * weights[4].shape[1] + width * pool_width)
    piece = (halves + (not aliased), 8, pool_width)
    out_shape = [jax.ShapeDtypeStruct((rows, width), BF), jax.ShapeDtypeStruct(piece, BF)]
    out_specs = [hbm, any_spec]
    scratch = [
        pltpu.VMEM((width, (windows + 1) * BLOCK), BF),
        pltpu.VMEM((points, width), BF),
        pltpu.VMEM((windows * TILE_PARENTS, CHILDREN * width), BF),
        pltpu.VMEM(piece, BF),
    ]
    scratch += [pltpu.VMEM(w.shape, BF) for w in weights]
    scratch += [
        pltpu.SemaphoreType.DMA((16,)),
        pltpu.SemaphoreType.DMA((7,)),
        pltpu.SemaphoreType.DMA((2,)),
        pltpu.SemaphoreType.DMA((1,)),
    ]
    if not aliased:
        ways = len(recv) + 1
        wide = (feat, (last_span[1] + 1) * BLOCK)
        out_shape += [jax.ShapeDtypeStruct(wide, BF)] * len(recv) + [jax.ShapeDtypeStruct((feat, BLOCK), BF)]
        out_specs += [any_spec] * ways
        scratch += [pltpu.VMEM(wide, BF)] * len(recv)
        scratch += [
            pltpu.VMEM((2, ways, feat, BLOCK), BF),
            pltpu.VMEM((ways, feat, BLOCK), BF),
            pltpu.SemaphoreType.DMA((2 * ways,)),
            pltpu.SemaphoreType.DMA((ways,)),
            pltpu.SemaphoreType.DMA((ways,)),
        ]
    return pl.pallas_call(
        functools.partial(chunk_kernel, spec),
        out_shape=tuple(out_shape),
        in_specs=[smem, smem] + [any_spec] * (moved - 2) + [hbm] * (len(args) - moved),
        out_specs=tuple(out_specs),
        scratch_shapes=scratch,
        input_output_aliases=aliases,
        compiler_params=pltpu.CompilerParams(vmem_limit_bytes=44 << 20),
        cost_estimate=pl.CostEstimate(
            flops=flops, transcendentals=points * 1024, bytes_accessed=points * width * 4 + (4 << 20)
        ),
        name=f"layer_chunk_{first_window}",
    )(*args[:moved], *in_hbm(args[moved:]))


def in_hbm(arrays):
    return [pltpu.with_memory_space_constraint(a, pltpu.HBM) for a in arrays]


def copy_run(piece, out, lower, size, first, limit, shift):
    def one(v, carry):
        out[v + shift] = piece[v - lower]
        return carry

    lax.fori_loop(jnp.maximum(first, lower), jnp.minimum(limit, lower + size), one, 0)


def place_kernel(kept_ref, *refs):
    count = (len(refs) - 3) // 2
    pieces_hbm, out_hbm, bufs, out, sems = (
        refs[:count],
        refs[count],
        refs[count + 1 : 2 * count + 1],
        refs[2 * count + 1],
        refs[2 * count + 2],
    )
    loads = [pltpu.make_async_copy(pieces_hbm[n], bufs[n], sems.at[n]) for n in range(count)]
    for c in loads:
        c.start()
    for c in loads:
        c.wait()
    own, came = bufs[: (count + 1) // 2], bufs[(count + 1) // 2 :]
    slots = out.shape[0]
    total = slots // 2
    kept = kept_ref[0] * 2
    kept_before = jnp.max(came[0][came[0].shape[0] - 1].astype(F32)).astype(jnp.int32) * 2
    blank = jnp.zeros(out.shape[1:], BF)

    def clear(v, carry):
        out[v] = blank
        return carry

    lax.fori_loop(kept + total - kept_before, slots, clear, 0)
    lower = 1
    for n, piece in enumerate(own):
        size = piece.shape[0] - (n == 0)
        copy_run(piece, out, lower, size, 0, jnp.minimum(kept, total), 0)
        lower += size
    lower = 1
    for n, piece in enumerate(came):
        size = piece.shape[0] - (n == 0)
        copy_run(piece, out, lower, size, kept_before, total, kept - kept_before)
        lower += size

    @pl.when(kept > 0)
    def _():
        out[0] = own[-1][own[-1].shape[0] - 1]

    c = pltpu.make_async_copy(out, out_hbm, sems.at[count])
    c.start()
    c.wait()


def final_kernel(kept_ref, piece, mark, _, out, sem):
    total = out.shape[0] // 2
    count = piece.shape[0]
    lower = total - (count - 3)
    kept = kept_ref[0] * 2
    kept_before = jnp.max(mark[mark.shape[0] - 1].astype(F32)).astype(jnp.int32) * 2
    shift = kept - kept_before

    def put(v, source):
        return pltpu.make_async_copy(piece.at[source], out.at[v + shift], sem.at[v])

    def start(v, carry):
        put(v, v - lower).start()
        return carry

    def wait(v, carry):
        put(v, v - lower).wait()
        return carry

    low = jnp.maximum(kept_before, lower)
    lax.fori_loop(low, total, start, 0)

    @pl.when(kept_before == 0)
    def _():
        put(0, count - 1).start()

    lax.fori_loop(low, total, wait, 0)

    @pl.when(kept_before == 0)
    def _():
        put(0, count - 1).wait()


def body(points, w_query, w_key, w_value, w_out, w_up, w_down, w_pool, keep_count):
    feat = points.shape[1]
    ways = lax.axis_size("mp")
    seq_ways = lax.axis_size("seq")
    quarter = points.shape[0] // ways
    pool_width = w_pool.shape[1]
    mp_index = lax.axis_index("mp").astype(jnp.int32)[None]
    own = points.T
    tiles_quarter = quarter // BLOCK
    last_chunk = len(CHUNKS) - 1

    spans = []
    tile = 0
    for n, windows in enumerate(CHUNKS):
        count = windows + 1 if n == 0 else windows
        if n == last_chunk:
            count = tiles_quarter - tile
        spans.append((tile, count))
        tile += count

    def exchange(block, shift):
        return lax.ppermute(block, "mp", [(i, i ^ shift) for i in range(ways)])

    edges = [(None, 0, 1), (None, own.shape[1] // BLOCK - 1, 1)]
    blocks = send_blocks(mp_index, own, quarter, [(s, *spans[0]) for s in SHIFTS] + edges, "first_blocks")
    received = [[exchange(b, s) for b, s in zip(blocks, SHIFTS)]]
    after = lax.ppermute(blocks[-2], "seq", [((i + 1) % seq_ways, i) for i in range(seq_ways)])
    prior = lax.ppermute(blocks[-1], "seq", [(i, (i + 1) % seq_ways) for i in range(seq_ways)])
    for n in range(1, last_chunk):
        blocks = send_blocks(mp_index, own, quarter, [(s, *spans[n]) for s in SHIFTS], f"blocks_{n}")
        received.append([exchange(b, s) for b, s in zip(blocks, SHIFTS)])

    pairs = [(i, (i + 1) % (seq_ways * ways)) for i in range(seq_ways * ways)]
    weights = [w_query, w_key, w_value, w_out, w_up, w_down, w_pool]
    refined = halo_own = None
    window = 1
    own_pooled, came_pooled = [], []
    for n, windows in enumerate(CHUNKS):
        tile, count = spans[n]
        spec = (tile, count, window, windows, n == last_chunk, n > 0, quarter, feat, spans[last_chunk])
        refined, pooled, *rest = run_chunk(
            spec,
            mp_index,
            keep_count,
            own,
            received[n],
            received[n - 1] if n else None,
            halo_own,
            received[0],
            came_pooled[0] if n else None,
            [after, prior],
            weights,
            refined,
            quarter,
        )
        own_pooled.append(pooled)
        came_pooled.append(lax.ppermute(pooled, ("seq", "mp"), pairs))
        window += windows
        if n == 0:
            halo_own = rest[-1]
            received.append([exchange(b, s) for b, s in zip(rest, SHIFTS)])

    slots = 2 * quarter // (CHILDREN * 8)
    smem = pl.BlockSpec(memory_space=pltpu.SMEM)
    hbm = pl.BlockSpec(memory_space=pltpu.HBM)
    vmem = pl.BlockSpec(memory_space=pltpu.VMEM)
    shape = (slots, 8, pool_width)
    pieces = own_pooled + came_pooled[:-1]
    coarse = pl.pallas_call(
        place_kernel,
        out_shape=jax.ShapeDtypeStruct(shape, BF),
        in_specs=[smem] + [pl.BlockSpec(memory_space=pl.ANY)] * len(pieces),
        out_specs=hbm,
        scratch_shapes=[pltpu.VMEM(p.shape, BF) for p in pieces]
        + [pltpu.VMEM(shape, BF), pltpu.SemaphoreType.DMA((len(pieces) + 1,))],
        compiler_params=pltpu.CompilerParams(vmem_limit_bytes=16 << 20),
        name="place_tiles",
    )(keep_count, *pieces)
    coarse = pl.pallas_call(
        final_kernel,
        out_shape=jax.ShapeDtypeStruct(shape, BF),
        in_specs=[smem, vmem, vmem, hbm],
        out_specs=hbm,
        scratch_shapes=[pltpu.SemaphoreType.DMA((slots // 2,))],
        input_output_aliases={3: 0},
        name="place_final",
    )(
        keep_count,
        pltpu.with_memory_space_constraint(came_pooled[-1], pltpu.VMEM),
        pltpu.with_memory_space_constraint(came_pooled[0], pltpu.VMEM),
        *in_hbm([coarse]),
    )
    return (refined, coarse.reshape(slots * 8, pool_width))


def solution(mesh):
    placed = (
        P(("groups", "seq"), "mp"),
        P(),
        P(),
        P(),
        P(),
        P(),
        P(),
        P(),
        P(("groups", "seq", "mp")),
    )
    return jax.shard_map(
        body,
        mesh=mesh,
        in_specs=placed,
        out_specs=(P(("groups", "seq", "mp"), None), P(("groups", "seq", "mp"), None)),
        check_vma=False,
    )
```

time: 89.3 us -> 60.5 us (0.68)
  local copies, waits for them, and re-layouts: 11.4 us -> 0 us
  Pallas kernels: 48.6 us -> 38.6 us
  other arithmetic: 4.54 us -> 0 us
  starting transfers between devices: 16.3 us -> 13 us
  waiting for transfers between devices: 6.21 us -> 7.12 us
    pallas_call x5 -> x7, Pallas kernels: 48.6 us -> 38.6 us  [the longest x3 30.6 us: run_chunk(): pl.pallas_call(functools.partial(chunk_kernel, spec), out_shape=tuple(out...]
    unnamed x22 -> x0, local copies, waits for them, and re-layouts: 5.33 us -> none
    dynamic_slice x3 -> x0, local copies, waits for them, and re-layouts: 3.66 us -> none  [body(): lax.dynamic_slice_in_dim(own, dest * quarter + tile * BLOCK, count * BLOC...]
    concatenate x4 -> x0, other arithmetic: 3.17 us -> none  [the longest x3 2.54 us: body(): block = jnp.concatenate([block, halo], axis=1)]
    ppermute x15 -> x11, starting transfers between devices: 13.9 us -> 11.3 us  [the longest x9 7.47 us: exchange(): return lax.ppermute(block, 'mp', [(i, i ^ shift) for i in range(ways)])]
    ppermute x15 -> x11, waiting for transfers between devices: 0.34 us -> 2.23 us  [the longest x1 2.21 us: body(): lax.ppermute(blocks[-1], 'seq', [(i, (i + 1) % seq_ways) for i in range(s...]
    slice x1 -> x0, local copies, waits for them, and re-layouts: 1.51 us -> none  [body(): final = own[:, own.shape[1] - BLOCK:]]
    ppermute x4 -> x3, waiting for transfers between devices: 5.87 us -> 4.89 us  [body(): came_pooled.append(lax.ppermute(pooled, ('seq', 'mp'), pairs))]
  transfers between devices with their start and end apart: 19 -> 14, of which waited for: 2 -> 2; matrix products, arithmetic and copies ran while one was open for 12% -> 0% of each run, Pallas kernels for 52% -> 59%
where the time goes in v1:
time: 60.5 us; the launch traced here: 60.3 us
  Pallas kernels  38.6 us (64%)
  starting transfers between devices  13 us (21%)
  waiting for transfers between devices  7.12 us (12%)
  between operations  1.55 us (3%)
    pallas_call x3, Pallas kernels, run_chunk(): pl.pallas_call(functools.partial(chunk_kernel, spec), out_shape=tuple(out...  30.6 us
    ppermute x9, starting transfers between devices, exchange(): return lax.ppermute(block, 'mp', [(i, i ^ shift) for i in range(ways)])  7.47 us
    ppermute x3, waiting for transfers between devices, body(): came_pooled.append(lax.ppermute(pooled, ('seq', 'mp'), pairs))  4.89 us
    ppermute x1, starting transfers between devices, body(): lax.ppermute(blocks[-2], 'seq', [((i + 1) % seq_ways, i) for i in range(s...  3.85 us
    pallas_call x2, Pallas kernels, send_blocks(): pl.pallas_call(functools.partial(send_kernel, quarter, wanted), out_shape...  3.66 us
    pallas_call x1, Pallas kernels, body(): pl.pallas_call(place_kernel, out_shape=jax.ShapeDtypeStruct(shape, BF), i...  2.88 us
    ppermute x1, waiting for transfers between devices, body(): lax.ppermute(blocks[-1], 'seq', [(i, (i + 1) % seq_ways) for i in range(s...  2.21 us
    ppermute x3, starting transfers between devices, body(): came_pooled.append(lax.ppermute(pooled, ('seq', 'mp'), pairs))  1.68 us
  transfers between devices with their start and end apart: 14, of which 2 were waited for; matrix products, arithmetic and copies ran while one was open for 0% of the time, Pallas kernels for 59%

profile of v1, /device:TPU:0, one launch (start us, length us, event | category | flops | bytes accessed | tf_op | source)
XLA Modules:
  0.0 60.3 jit_solution(442811592886689359)
XLA Ops:
  0.6 1.8 %first_blocks.1 = (bf16[64,1024]{1,0:T(8,128)(2,1)}, bf16[64,1024]{1,0:T(8,128)(2,1)}, bf16[64,1024]{1,0:T(8,128)(2,1)}, bf16[64,128]{1,0:T(8,128)(2,1)}, bf16[64,128]{1,0:T(8,128)(2,1)}) custom-call(s32[1]{0:T(128)} %bitcast.mp_ref.refs_0_, bf16[64,16384]{1,0:T(8,128)(2,1)} %bitcast.3), custom_call_target="tpu_custom_call" | custom-call | tf_op jit(solution)/shard_map/first_blocks/pallas_call | solution.py:148
  2.4 2.4 %collective-permute-start = (bf16[64,1024]{1,0:T(8,128)(2,1)}, bf16[64,1024]{1,0:T(8,128)(2,1)S(1)}, u32[]{:S(2)}, u32[]{:S(2)}) collective-permute-start(bf16[64,1024]{1,0:T(8,128)(2,1)} %get-tuple-element.20), channel_id=1, source_target_pairs={{0,3},{1,2},{2,1},{3,0},{4,7},{5,6},{6,5},{7,4},{8,11},{9,10},{10,... | collective-permute-start | bytes 393224 | tf_op jit(solution)/shard_map/ppermute | solution.py:489
  4.9 0.6 %collective-permute-start.1 = (bf16[64,1024]{1,0:T(8,128)(2,1)}, bf16[64,1024]{1,0:T(8,128)(2,1)S(1)}, u32[]{:S(2)}, u32[]{:S(2)}) collective-permute-start(bf16[64,1024]{1,0:T(8,128)(2,1)} %get-tuple-element.21), channel_id=1, source_target_pairs={{0,2},{1,3},{2,0},{3,1},{4,6},{5,7},{6,4},{7,5},{8,10},{9,11},{10,... | collective-permute-start | bytes 393224 | tf_op jit(solution)/shard_map/ppermute | solution.py:489
  5.5 0.0 collective-permute-start.2
  5.5 3.9 %collective-permute-start.3 = (bf16[64,128]{1,0:T(8,128)(2,1)}, bf16[64,128]{1,0:T(8,128)(2,1)S(1)}, u32[]{:S(2)}, u32[]{:S(2)}) collective-permute-start(bf16[64,128]{1,0:T(8,128)(2,1)} %get-tuple-element.23), channel_id=1, source_target_pairs={{4,0},{8,4},{12,8},{0,12},{5,1},{9,5},{13,9},{1,13},{6,2},{10,6},{... | collective-permute-start | bytes 49160 | tf_op jit(solution)/shard_map/ppermute | solution.py:494
  9.4 0.0 collective-permute-start.4
  9.4 1.9 %blocks_1.1 = (bf16[64,1664]{1,0:T(8,128)(2,1)}, bf16[64,1664]{1,0:T(8,128)(2,1)}, bf16[64,1664]{1,0:T(8,128)(2,1)}) custom-call(s32[1]{0:T(128)} %bitcast.mp_ref.refs_0_, bf16[64,16384]{1,0:T(8,128)(2,1)} %bitcast.4), custom_call_target="tpu_custom_call" | custom-call | tf_op jit(solution)/shard_map/blocks_1/pallas_call | solution.py:148
  11.9 0.0 collective-permute-done.3.refs_6_
  11.9 1.0 %collective-permute-start.8 = (bf16[64,1664]{1,0:T(8,128)(2,1)}, bf16[64,1664]{1,0:T(8,128)(2,1)S(1)}, u32[]{:S(2)}, u32[]{:S(2)}) collective-permute-start(bf16[64,1664]{1,0:T(8,128)(2,1)} %get-tuple-element.28), channel_id=1, source_target_pairs={{0,3},{1,2},{2,1},{3,0},{4,7},{5,6},{6,5},{7,4},{8,11},{9,10},{10,... | collective-permute-start | bytes 638984 | tf_op jit(solution)/shard_map/ppermute | solution.py:489
  12.9 2.2 %collective-permute-done.4.refs_7_ = bf16[64,128]{1,0:T(8,128)(2,1)S(1)} collective-permute-done((bf16[64,128]{1,0:T(8,128)(2,1)}, bf16[64,128]{1,0:T(8,128)(2,1)S(1)}, u32[]{:S(2)}, u32[]{:S(2)}) %collective-permute-start.4) | collective-permute-done | bytes 16416 | tf_op jit(solution)/shard_map/ppermute | solution.py:495
  15.1 1.5 %collective-permute-start.9 = (bf16[64,1664]{1,0:T(8,128)(2,1)}, bf16[64,1664]{1,0:T(8,128)(2,1)S(1)}, u32[]{:S(2)}, u32[]{:S(2)}) collective-permute-start(bf16[64,1664]{1,0:T(8,128)(2,1)} %get-tuple-element.29), channel_id=1, source_target_pairs={{0,2},{1,3},{2,0},{3,1},{4,6},{5,7},{6,4},{7,5},{8,10},{9,11},{10,... | collective-permute-start | bytes 638984 | tf_op jit(solution)/shard_map/ppermute | solution.py:489
  16.6 0.0 collective-permute-done.refs_3_.refs_6_.refs_10_
  16.6 0.0 collective-permute-start.10
  16.6 0.0 collective-permute-done.1.refs_4_.refs_7_.refs_11_
  16.7 0.0 collective-permute-done.2.refs_5_.refs_8_.refs_12_
  16.7 9.3 %layer_chunk_1.1 = (bf16[4096,256]{1,0:T(8,128)(2,1)}, bf16[15,8,512]{2,1,0:T(8,128)(2,1)S(1)}, bf16[64,1536]{1,0:T(8,128)(2,1)S(1)}, bf16[64,1536]{1,0:T(8,128)...) custom-call(s32[1]{0:T(128)} %bitcast.mp_ref.refs_0_, s32[1]{0:T(128)S(6)} %copy.17.refs_1_.kept_ref, ...), custom_call_target="tpu_custom_call" | custom-call | flops 3053453312 | bytes 5111808 | tf_op jit(solution)/shard_map/layer_chunk_1/pallas_call | solution.py:362
  26.0 0.7 %collective-permute-start.11 = (bf16[15,8,512]{2,1,0:T(8,128)(2,1)S(1)}, bf16[15,8,512]{2,1,0:T(8,128)(2,1)S(1)}, u32[]{:S(2)}, u32[]{:S(2)}) collective-permute-start(bf16[15,8,512]{2,1,0:T(8,128)(2,1)S(1)} %get-tuple-element.32.refs_0_), channel_id=1, source_target_pairs={{0,1},{1,2},{2,3},{3,4},{4,5},{5,6},{6,7},{7,8},{8,9},{9,10},{10,1... | collective-permute-start | bytes 368648 | tf_op jit(solution)/shard_map/ppermute | solution.py:524
  26.7 0.2 collective-permute-start.5
  26.9 0.0 collective-permute-done.8.refs_3_.refs_6_
  26.9 1.6 %collective-permute-start.6 = (bf16[64,1536]{1,0:T(8,128)(2,1)S(1)}, bf16[64,1536]{1,0:T(8,128)(2,1)S(1)}, u32[]{:S(2)}, u32[]{:S(2)}) collective-permute-start(bf16[64,1536]{1,0:T(8,128)(2,1)S(1)} %get-tuple-element.26), channel_id=1, source_target_pairs={{0,2},{1,3},{2,0},{3,1},{4,6},{5,7},{6,4},{7,5},{8,10},{9,11},{10,... | collective-permute-start | bytes 589832 | tf_op jit(solution)/shard_map/ppermute | solution.py:489
  28.5 0.0 collective-permute-done.9.refs_4_.refs_7_
  28.5 0.0 collective-permute-start.7
  28.5 0.0 collective-permute-done.10.refs_5_.refs_8_
  28.5 10.7 %layer_chunk_8.1 = (bf16[4096,256]{1,0:T(8,128)(2,1)}, bf16[26,8,512]{2,1,0:T(8,128)(2,1)S(1)}) custom-call(s32[1]{0:T(128)} %bitcast.mp_ref.refs_0_, s32[1]{0:T(128)S(6)} %copy.17.refs_1_.kept_ref, bf16[64,16384]{1,0:T(8,128)(2,1)} %bitcast.6, bf16[64,1664]{1,0:T(8,128)(2,1)S(1)} %collective-permute-done.8.refs_3_.refs_6_, ...), custom_call_target="tpu_custom_call", output_to_operand_aliasing={{0}: (16, {})} | custom-call | flops 5670699008 | bytes 5898240 | tf_op jit(solution)/shard_map/layer_chunk_8/pallas_call | solution.py:362
  39.3 0.7 %collective-permute-start.13 = (bf16[26,8,512]{2,1,0:T(8,128)(2,1)S(1)}, bf16[26,8,512]{2,1,0:T(8,128)(2,1)S(1)}, u32[]{:S(2)}, u32[]{:S(2)}) collective-permute-start(bf16[26,8,512]{2,1,0:T(8,128)(2,1)S(1)} %get-tuple-element.37.refs_1_), channel_id=1, source_target_pairs={{0,1},{1,2},{2,3},{3,4},{4,5},{5,6},{6,7},{7,8},{8,9},{9,10},{10,1... | collective-permute-start | bytes 638984 | tf_op jit(solution)/shard_map/ppermute | solution.py:524
  40.0 0.0 collective-permute-done.11.refs_13_.refs_3_.mark
  40.0 0.0 collective-permute-done.5.refs_3_
  40.0 0.0 collective-permute-done.6.refs_4_
  40.0 0.0 collective-permute-done.7.refs_5_
  40.0 10.6 %layer_chunk_21.1 = (bf16[4096,256]{1,0:T(8,128)(2,1)}, bf16[26,8,512]{2,1,0:T(8,128)(2,1)S(1)}) custom-call(s32[1]{0:T(128)} %bitcast.mp_ref.refs_0_, s32[1]{0:T(128)S(6)} %copy.17.refs_1_.kept_ref, bf16[64,16384]{1,0:T(8,128)(2,1)} %bitcast.7, bf16[64,1536]{1,0:T(8,128)(2,1)S(1)} %collective-permute-done.5.refs_3_, ...), custom_call_target="tpu_custom_call", output_to_operand_aliasing={{0}: (21, {})} | custom-call | flops 5670699008 | bytes 5898240 | tf_op jit(solution)/shard_map/layer_chunk_21/pallas_call | solution.py:362
  50.6 0.2 collective-permute-start.12
  50.9 0.0 collective-permute-done.13.refs_4_
  50.9 2.9 %place_tiles.1._ = bf16[128,8,512]{2,1,0:T(8,128)(2,1)} custom-call(s32[1]{0:T(128)S(6)} %copy.17.refs_1_.kept_ref, bf16[15,8,512]{2,1,0:T(8,128)(2,1)S(1)} %get-tuple-element.32.refs_0_, bf16[26,8,512]{2,1,0:T(8,128)(2,1)S(1)} %get-tuple-element.37.refs_1_, bf16[26,8,512]{2,1,0:T(8,128)(2,1)S(1)} %get-tuple-element.36.refs_2_, ...), custom_call_target="tpu_custom_call" | custom-call | tf_op jit(solution)/shard_map/place_tiles/pallas_call | solution.py:536
  53.8 4.9 %collective-permute-done.12.piece = bf16[26,8,512]{2,1,0:T(8,128)(2,1)S(1)} collective-permute-done((bf16[26,8,512]{2,1,0:T(8,128)(2,1)S(1)}, bf16[26,8,512]{2,1,0:T(8,128)(2,1)S(1)}, u32[]{:S(2)}, u32[]{:S(2)}) %collective-permute-start.12) | collective-permute-done | bytes 213024 | tf_op jit(solution)/shard_map/ppermute | solution.py:524
  58.7 1.4 %place_final.1 = bf16[128,8,512]{2,1,0:T(8,128)(2,1)} custom-call(s32[1]{0:T(128)S(6)} %copy.17.refs_1_.kept_ref, bf16[26,8,512]{2,1,0:T(8,128)(2,1)S(1)} %collective-permute-done.12.piece, bf16[15,8,512]{2,1,0:T(8,128)(2,1)S(1)} %collective-permute-done.11.refs_13_.refs_3_.mark, bf16[128,8,512]{2,1,0:T(8,128)(2,1)} %place_tiles.1._), custom_call_target="tpu_custom_call", output_to_operand_aliasing={{}: (3, {})} | custom-call | tf_op jit(solution)/shard_map/place_final/pallas_call | solution.py:546
Async XLA Ops:
  2.4 14.2 %collective-permute-start = (bf16[64,1024]{1,0:T(8,128)(2,1)}, bf16[64,1024]{1,0:T(8,128)(2,1)S(1)}, u32[]{:S(2)}, u32[]{:S(2)}) collective-permute-start(bf16[64,1024]{1,0:T(8,128)(2,1)} %get-tuple-element.20), channel_id=1, source_target_pairs={{0,3},{1,2},{2,1},{3,0},{4,7},{5,6},{6,5},{7,4},{8,11},{9,10},{10,... | collective-permute-start | bytes 393224 | tf_op jit(solution)/shard_map/ppermute | solution.py:489
  4.9 11.8 %collective-permute-start.1 = (bf16[64,1024]{1,0:T(8,128)(2,1)}, bf16[64,1024]{1,0:T(8,128)(2,1)S(1)}, u32[]{:S(2)}, u32[]{:S(2)}) collective-permute-start(bf16[64,1024]{1,0:T(8,128)(2,1)} %get-tuple-element.21), channel_id=1, source_target_pairs={{0,2},{1,3},{2,0},{3,1},{4,6},{5,7},{6,4},{7,5},{8,10},{9,11},{10,... | collective-permute-start | bytes 393224 | tf_op jit(solution)/shard_map/ppermute | solution.py:489
  5.5 11.1 %collective-permute-start.2 = (bf16[64,1024]{1,0:T(8,128)(2,1)}, bf16[64,1024]{1,0:T(8,128)(2,1)S(1)}, u32[]{:S(2)}, u32[]{:S(2)}) collective-permute-start(bf16[64,1024]{1,0:T(8,128)(2,1)} %get-tuple-element.22), channel_id=1, source_target_pairs={{0,1},{1,0},{2,3},{3,2},{4,5},{5,4},{6,7},{7,6},{8,9},{9,8},{10,11... | collective-permute-start | bytes 393224 | tf_op jit(solution)/shard_map/ppermute | solution.py:489
  5.5 6.4 %collective-permute-start.3 = (bf16[64,128]{1,0:T(8,128)(2,1)}, bf16[64,128]{1,0:T(8,128)(2,1)S(1)}, u32[]{:S(2)}, u32[]{:S(2)}) collective-permute-start(bf16[64,128]{1,0:T(8,128)(2,1)} %get-tuple-element.23), channel_id=1, source_target_pairs={{4,0},{8,4},{12,8},{0,12},{5,1},{9,5},{13,9},{1,13},{6,2},{10,6},{... | collective-permute-start | bytes 49160 | tf_op jit(solution)/shard_map/ppermute | solution.py:494
  9.4 5.7 %collective-permute-start.4 = (bf16[64,128]{1,0:T(8,128)(2,1)}, bf16[64,128]{1,0:T(8,128)(2,1)S(1)}, u32[]{:S(2)}, u32[]{:S(2)}) collective-permute-start(bf16[64,128]{1,0:T(8,128)(2,1)} %get-tuple-element.24), channel_id=1, source_target_pairs={{0,4},{4,8},{8,12},{12,0},{1,5},{5,9},{9,13},{13,1},{2,6},{6,10},{... | collective-permute-start | bytes 49160 | tf_op jit(solution)/shard_map/ppermute | solution.py:495
  11.9 14.9 %collective-permute-start.8 = (bf16[64,1664]{1,0:T(8,128)(2,1)}, bf16[64,1664]{1,0:T(8,128)(2,1)S(1)}, u32[]{:S(2)}, u32[]{:S(2)}) collective-permute-start(bf16[64,1664]{1,0:T(8,128)(2,1)} %get-tuple-element.28), channel_id=1, source_target_pairs={{0,3},{1,2},{2,1},{3,0},{4,7},{5,6},{6,5},{7,4},{8,11},{9,10},{10,... | collective-permute-start | bytes 638984 | tf_op jit(solution)/shard_map/ppermute | solution.py:489
  15.1 13.3 %collective-permute-start.9 = (bf16[64,1664]{1,0:T(8,128)(2,1)}, bf16[64,1664]{1,0:T(8,128)(2,1)S(1)}, u32[]{:S(2)}, u32[]{:S(2)}) collective-permute-start(bf16[64,1664]{1,0:T(8,128)(2,1)} %get-tuple-element.29), channel_id=1, source_target_pairs={{0,2},{1,3},{2,0},{3,1},{4,6},{5,7},{6,4},{7,5},{8,10},{9,11},{10,... | collective-permute-start | bytes 638984 | tf_op jit(solution)/shard_map/ppermute | solution.py:489
  16.6 11.9 %collective-permute-start.10 = (bf16[64,1664]{1,0:T(8,128)(2,1)}, bf16[64,1664]{1,0:T(8,128)(2,1)S(1)}, u32[]{:S(2)}, u32[]{:S(2)}) collective-permute-start(bf16[64,1664]{1,0:T(8,128)(2,1)} %get-tuple-element.30), channel_id=1, source_target_pairs={{0,1},{1,0},{2,3},{3,2},{4,5},{5,4},{6,7},{7,6},{8,9},{9,8},{10,11... | collective-permute-start | bytes 638984 | tf_op jit(solution)/shard_map/ppermute | solution.py:489
  26.0 14.0 %collective-permute-start.11 = (bf16[15,8,512]{2,1,0:T(8,128)(2,1)S(1)}, bf16[15,8,512]{2,1,0:T(8,128)(2,1)S(1)}, u32[]{:S(2)}, u32[]{:S(2)}) collective-permute-start(bf16[15,8,512]{2,1,0:T(8,128)(2,1)S(1)} %get-tuple-element.32.refs_0_), channel_id=1, source_target_pairs={{0,1},{1,2},{2,3},{3,4},{4,5},{5,6},{6,7},{7,8},{8,9},{9,10},{10,1... | collective-permute-start | bytes 368648 | tf_op jit(solution)/shard_map/ppermute | solution.py:524
  26.7 13.3 %collective-permute-start.5 = (bf16[64,1536]{1,0:T(8,128)(2,1)S(1)}, bf16[64,1536]{1,0:T(8,128)(2,1)S(1)}, u32[]{:S(2)}, u32[]{:S(2)}) collective-permute-start(bf16[64,1536]{1,0:T(8,128)(2,1)S(1)} %get-tuple-element.25), channel_id=1, source_target_pairs={{0,3},{1,2},{2,1},{3,0},{4,7},{5,6},{6,5},{7,4},{8,11},{9,10},{10,... | collective-permute-start | bytes 589832 | tf_op jit(solution)/shard_map/ppermute | solution.py:489
  26.9 13.1 %collective-permute-start.6 = (bf16[64,1536]{1,0:T(8,128)(2,1)S(1)}, bf16[64,1536]{1,0:T(8,128)(2,1)S(1)}, u32[]{:S(2)}, u32[]{:S(2)}) collective-permute-start(bf16[64,1536]{1,0:T(8,128)(2,1)S(1)} %get-tuple-element.26), channel_id=1, source_target_pairs={{0,2},{1,3},{2,0},{3,1},{4,6},{5,7},{6,4},{7,5},{8,10},{9,11},{10,... | collective-permute-start | bytes 589832 | tf_op jit(solution)/shard_map/ppermute | solution.py:489
  28.5 11.5 %collective-permute-start.7 = (bf16[64,1536]{1,0:T(8,128)(2,1)S(1)}, bf16[64,1536]{1,0:T(8,128)(2,1)S(1)}, u32[]{:S(2)}, u32[]{:S(2)}) collective-permute-start(bf16[64,1536]{1,0:T(8,128)(2,1)S(1)} %get-tuple-element.27), channel_id=1, source_target_pairs={{0,1},{1,0},{2,3},{3,2},{4,5},{5,4},{6,7},{7,6},{8,9},{9,8},{10,11... | collective-permute-start | bytes 589832 | tf_op jit(solution)/shard_map/ppermute | solution.py:489
  39.3 11.6 %collective-permute-start.13 = (bf16[26,8,512]{2,1,0:T(8,128)(2,1)S(1)}, bf16[26,8,512]{2,1,0:T(8,128)(2,1)S(1)}, u32[]{:S(2)}, u32[]{:S(2)}) collective-permute-start(bf16[26,8,512]{2,1,0:T(8,128)(2,1)S(1)} %get-tuple-element.37.refs_1_), channel_id=1, source_target_pairs={{0,1},{1,2},{2,3},{3,4},{4,5},{5,6},{6,7},{7,8},{8,9},{9,10},{10,1... | collective-permute-start | bytes 638984 | tf_op jit(solution)/shard_map/ppermute | solution.py:524
  50.6 8.0 %collective-permute-start.12 = (bf16[26,8,512]{2,1,0:T(8,128)(2,1)S(1)}, bf16[26,8,512]{2,1,0:T(8,128)(2,1)S(1)}, u32[]{:S(2)}, u32[]{:S(2)}) collective-permute-start(bf16[26,8,512]{2,1,0:T(8,128)(2,1)S(1)} %get-tuple-element.36.refs_2_), channel_id=1, source_target_pairs={{0,1},{1,2},{2,3},{3,4},{4,5},{5,6},{6,7},{7,8},{8,9},{9,10},{10,1... | collective-permute-start | bytes 638984 | tf_op jit(solution)/shard_map/ppermute | solution.py:524

commit v2 on v1

--- a/solution.py
+++ b/solution.py
@@ -128,12 +128,13 @@
     count = len(wanted)
     outs, bufs, sems = refs[:count], refs[count : 2 * count], refs[2 * count]
     loads, puts = [], []
-    for n, (shift, tile, tiles) in enumerate(wanted):
+    for n, (shift, tile, tiles, free) in enumerate(wanted):
         col = tile * BLOCK
         if shift is not None:
             col = pl.multiple_of((mp_ref[0] ^ shift) * quarter + col, BLOCK)
         loads.append(pltpu.make_async_copy(own.at[:, pl.ds(col, tiles * BLOCK)], bufs[n], sems.at[0, n]))
-        puts.append(pltpu.make_async_copy(bufs[n], outs[n], sems.at[1, n]))
+        dst = outs[n].at[:, pl.ds(0, tiles * BLOCK)] if free else outs[n]
+        puts.append(pltpu.make_async_copy(bufs[n], dst, sems.at[1, n]))
     for c in loads:
         c.start()
     for load, put in zip(loads, puts):
@@ -147,41 +148,38 @@
     hbm = pl.BlockSpec(memory_space=pltpu.HBM)
     return pl.pallas_call(
         functools.partial(send_kernel, quarter, wanted),
-        out_shape=tuple(jax.ShapeDtypeStruct((own.shape[0], t * BLOCK), BF) for _, _, t in wanted),
+        out_shape=tuple(jax.ShapeDtypeStruct((own.shape[0], (t + f) * BLOCK), BF) for _, _, t, f in wanted),
         in_specs=[pl.BlockSpec(memory_space=pltpu.SMEM), hbm],
         out_specs=(hbm,) * len(wanted),
-        scratch_shapes=[pltpu.VMEM((own.shape[0], t * BLOCK), BF) for _, _, t in wanted]
+        scratch_shapes=[pltpu.VMEM((own.shape[0], t * BLOCK), BF) for _, _, t, _ in wanted]
         + [pltpu.SemaphoreType.DMA((2, len(wanted)))],
         name=name,
     )(mp_index, *in_hbm([own]))
 
 
-def last_blocks(spec, mp_index, own, after, prior, outs, bufs, edge, halo, edge_sems, load_sems, put_sems):
-    quarter, ways, tile, tiles = spec
-    edges, loads = [], []
+def last_blocks(spec, mp_index, own, after, prior, outs, edge, halo, edge_sems, put_sems):
+    quarter, ways, tiles = spec
+    edges = []
     for q in range(ways):
         head = own.at[:, pl.ds((q + 1) * quarter, BLOCK)] if q + 1 < ways else after
         tail = own.at[:, pl.ds(q * quarter - BLOCK, BLOCK)] if q else prior
         edges.append(pltpu.make_async_copy(head, edge.at[0, q], edge_sems.at[2 * q]))
         edges.append(pltpu.make_async_copy(tail, edge.at[1, q], edge_sems.at[2 * q + 1]))
+    puts = []
     for n in range(ways - 1):
-        col = pl.multiple_of((mp_index ^ SHIFTS[n]) * quarter + tile * BLOCK, BLOCK)
-        dst = bufs[n].at[:, pl.ds(0, tiles * BLOCK)]
-        loads.append(pltpu.make_async_copy(own.at[:, pl.ds(col, tiles * BLOCK)], dst, load_sems.at[n]))
-    puts = [pltpu.make_async_copy(bufs[n], outs[n], put_sems.at[n]) for n in range(ways - 1)]
+        dst = outs[n].at[:, pl.ds(tiles * BLOCK, BLOCK)]
+        puts.append(pltpu.make_async_copy(halo.at[mp_index ^ SHIFTS[n]], dst, put_sems.at[n]))
     puts.append(pltpu.make_async_copy(halo.at[mp_index], outs[ways - 1], put_sems.at[ways - 1]))
 
     def begin():
-        for c in edges + loads:
+        for c in edges:
             c.start()
 
     def send():
-        for c in edges + loads:
+        for c in edges:
             c.wait()
         lane = lax.broadcasted_iota(jnp.int32, edge.shape[1:], 2)
         halo[...] = jnp.where(lane < HALF, edge[0].astype(F32), edge[1].astype(F32)).astype(BF)
-        for n in range(ways - 1):
-            bufs[n][:, tiles * BLOCK :] = halo[mp_index ^ SHIFTS[n]]
         for c in puts:
             c.start()
 
@@ -193,7 +191,7 @@
 
 
 def chunk_kernel(spec, *refs):
-    first_tile, tiles, first_window, windows, last, aliased, quarter, feat, last_span = spec
+    first_tile, tiles, first_window, windows, last, aliased, marked, quarter, feat, last_span = spec
     n_recv = 3
     it = iter(refs)
     place_ref = next(it)
@@ -205,9 +203,12 @@
     if last:
         halo_own = next(it)
         start = [next(it) for _ in range(n_recv)]
-        next(it)
+    elif aliased:
+        pooled_before = next(it)
     if not aliased:
         after, prior = next(it), next(it)
+        for _ in range(n_recv):
+            next(it)
     weights_hbm = [next(it) for _ in range(7)]
     if aliased:
         next(it)
@@ -219,16 +220,18 @@
     in_sem, w_sem, out_sem, pool_sem = (next(it) for _ in range(4))
     mp_index = place_ref[0]
     if not aliased:
-        block_bufs = [next(it) for _ in range(n_recv)]
         begin, send, end = last_blocks(
-            (quarter, n_recv + 1) + last_span, mp_index, own, after, prior, block_outs, block_bufs, *it
+            (quarter, n_recv + 1, last_span[1]), mp_index, own, after, prior, block_outs, *it
         )
     copies = []
+    kept_halves = pooled_before.shape[0] if aliased and not last else 0
     fetch = [pltpu.make_async_copy(weights_hbm[n], weights[n], w_sem.at[n]) for n in range(7)]
 
     def arrive(first, limit):
         for n in range(first, limit):
             fetch[n].wait()
+        if first == 3 and not aliased:
+            send()
 
     def bring(src, shift, col, width):
         j = mp_index ^ shift
@@ -265,6 +268,9 @@
         fetch[n].start()
     if not aliased:
         begin()
+    if kept_halves:
+        carried = pltpu.make_async_copy(pooled_before, pooled_buf.at[pl.ds(0, kept_halves)], pool_sem.at[1])
+        carried.start()
 
     width = 4 * feat
     xs = [dot_nt(gather, xbuf[:, n * BLOCK : (n + 2) * BLOCK]) for n in range(windows)]
@@ -275,8 +281,6 @@
         for c in range(CHILDREN):
             piece = both[BLOCK + c * TILE_PARENTS : BLOCK + (c + 1) * TILE_PARENTS]
             pbuf[n * TILE_PARENTS : (n + 1) * TILE_PARENTS, c * width : (c + 1) * width] = piece
-    if not aliased:
-        send()
     base = first_window * BLOCK - HALF
     outs = []
     if last:
@@ -295,9 +299,12 @@
     arrive(6, 7)
     result = dot_nn(pbuf[...], weights[6][...])
     halves = windows * TILE_PARENTS // 8
-    pooled_buf[:halves] = result.reshape((halves,) + pooled_buf.shape[1:]).astype(BF)
-    if not aliased:
-        pooled_buf[halves] = jnp.full(pooled_buf.shape[1:], kept_ref[0], jnp.int32).astype(F32).astype(BF)
+    result = result.reshape((halves,) + pooled_buf.shape[1:]).astype(BF)
+    pooled_buf[kept_halves : kept_halves + halves] = result
+    if marked:
+        pooled_buf[kept_halves + halves] = jnp.full(pooled_buf.shape[1:], kept_ref[0], jnp.int32).astype(F32).astype(BF)
+    if kept_halves:
+        carried.wait()
     c = pltpu.make_async_copy(pooled_buf, pooled, pool_sem.at[0])
     c.start()
     c.wait()
@@ -307,8 +314,8 @@
         end()
 
 
-def run_chunk(spec, mp_index, kept, own, recv, before, halo_own, start, tied, edges, weights, refined, rows):
-    first_tile, tiles, first_window, windows, last, aliased, quarter, feat, last_span = spec
+def run_chunk(spec, mp_index, kept, own, recv, before, halo_own, start, pooled_before, edges, weights, refined, rows):
+    first_tile, tiles, first_window, windows, last, aliased, marked, quarter, feat, last_span = spec
     width = 4 * feat
     pool_width = weights[6].shape[1]
     smem = pl.BlockSpec(memory_space=pltpu.SMEM)
@@ -318,19 +325,25 @@
     if first_window > 1:
         args += before
     if last:
-        args += [halo_own] + start + [tied]
-    if not aliased:
-        args += edges
+        args += [halo_own] + start
+    elif aliased:
+        args.append(pooled_before)
+    aliases = {}
+    if not aliased:
+        args += edges[:2]
+        for n, block in enumerate(in_hbm(edges[2:])):
+            aliases[len(args)] = 2 + n
+            args.append(block)
     moved = len(args)
     args += weights
-    aliases = {}
     if aliased:
         aliases = {len(args): 0}
         args.append(refined)
     halves = windows * TILE_PARENTS // 8
     points = windows * BLOCK
     flops = 2 * points * (width * width * 16 + 2 * width * weights[4].shape[1] + width * pool_width)
-    piece = (halves + (not aliased), 8, pool_width)
+    before_halves = pooled_before.shape[0] if aliased and not last else 0
+    piece = (before_halves + halves + int(marked), 8, pool_width)
     out_shape = [jax.ShapeDtypeStruct((rows, width), BF), jax.ShapeDtypeStruct(piece, BF)]
     out_specs = [hbm, any_spec]
     scratch = [
@@ -344,19 +357,17 @@
         pltpu.SemaphoreType.DMA((16,)),
         pltpu.SemaphoreType.DMA((7,)),
         pltpu.SemaphoreType.DMA((2,)),
-        pltpu.SemaphoreType.DMA((1,)),
+        pltpu.SemaphoreType.DMA((2,)),
     ]
     if not aliased:
         ways = len(recv) + 1
         wide = (feat, (last_span[1] + 1) * BLOCK)
         out_shape += [jax.ShapeDtypeStruct(wide, BF)] * len(recv) + [jax.ShapeDtypeStruct((feat, BLOCK), BF)]
-        out_specs += [any_spec] * ways
-        scratch += [pltpu.VMEM(wide, BF)] * len(recv)
+        out_specs += [hbm] * len(recv) + [any_spec]
         scratch += [
             pltpu.VMEM((2, ways, feat, BLOCK), BF),
             pltpu.VMEM((ways, feat, BLOCK), BF),
             pltpu.SemaphoreType.DMA((2 * ways,)),
-            pltpu.SemaphoreType.DMA((ways,)),
             pltpu.SemaphoreType.DMA((ways,)),
         ]
     return pl.pallas_call(
@@ -488,23 +499,25 @@
     def exchange(block, shift):
         return lax.ppermute(block, "mp", [(i, i ^ shift) for i in range(ways)])
 
-    edges = [(None, 0, 1), (None, own.shape[1] // BLOCK - 1, 1)]
-    blocks = send_blocks(mp_index, own, quarter, [(s, *spans[0]) for s in SHIFTS] + edges, "first_blocks")
+    edges = [(None, 0, 1, 0), (None, own.shape[1] // BLOCK - 1, 1, 0)]
+    blocks = send_blocks(mp_index, own, quarter, [(s, *spans[0], 0) for s in SHIFTS] + edges, "first_blocks")
     received = [[exchange(b, s) for b, s in zip(blocks, SHIFTS)]]
     after = lax.ppermute(blocks[-2], "seq", [((i + 1) % seq_ways, i) for i in range(seq_ways)])
     prior = lax.ppermute(blocks[-1], "seq", [(i, (i + 1) % seq_ways) for i in range(seq_ways)])
-    for n in range(1, last_chunk):
-        blocks = send_blocks(mp_index, own, quarter, [(s, *spans[n]) for s in SHIFTS], f"blocks_{n}")
-        received.append([exchange(b, s) for b, s in zip(blocks, SHIFTS)])
+    wanted = [(s, *spans[n], int(n == last_chunk)) for n in range(1, last_chunk + 1) for s in SHIFTS]
+    blocks = list(send_blocks(mp_index, own, quarter, wanted, "later_blocks"))
+    for n in range(last_chunk - 1):
+        received.append([exchange(blocks[n * len(SHIFTS) + m], s) for m, s in enumerate(SHIFTS)])
+    unfinished = blocks[-len(SHIFTS) :]
 
     pairs = [(i, (i + 1) % (seq_ways * ways)) for i in range(seq_ways * ways)]
     weights = [w_query, w_key, w_value, w_out, w_up, w_down, w_pool]
-    refined = halo_own = None
+    refined = halo_own = pooled = None
     window = 1
     own_pooled, came_pooled = [], []
     for n, windows in enumerate(CHUNKS):
         tile, count = spans[n]
-        spec = (tile, count, window, windows, n == last_chunk, n > 0, quarter, feat, spans[last_chunk])
+        spec = (tile, count, window, windows, n == last_chunk, n > 0, n == last_chunk - 1, quarter, feat, spans[last_chunk])
         refined, pooled, *rest = run_chunk(
             spec,
             mp_index,
@@ -514,14 +527,15 @@
             received[n - 1] if n else None,
             halo_own,
             received[0],
-            came_pooled[0] if n else None,
-            [after, prior],
+            pooled,
+            [after, prior] + unfinished,
             weights,
             refined,
             quarter,
         )
-        own_pooled.append(pooled)
-        came_pooled.append(lax.ppermute(pooled, ("seq", "mp"), pairs))
+        if n >= last_chunk - 1:
+            own_pooled.append(pooled)
+            came_pooled.append(lax.ppermute(pooled, ("seq", "mp"), pairs))
         window += windows
         if n == 0:
             halo_own = rest[-1]

time: 60.5 us -> 59.1 us (0.977)
  Pallas kernels: 38.6 us -> 37.7 us
    ppermute x3 -> x2, starting transfers between devices: 1.68 us -> 0.76 us  [body(): came_pooled.append(lax.ppermute(pooled, ('seq', 'mp'), pairs))]
    ppermute x3 -> x2, waiting for transfers between devices: 4.89 us -> 5.48 us  [body(): came_pooled.append(lax.ppermute(pooled, ('seq', 'mp'), pairs))]
  transfers between devices with their start and end apart: 14 -> 13, of which waited for: 2 -> 2; matrix products, arithmetic and copies ran while one was open for 0% -> 0% of each run, Pallas kernels for 59% -> 58%
where the time goes in v2:
time: 59.1 us
  Pallas kernels  37.7 us (64%)
  starting transfers between devices  12.4 us (21%)
  waiting for transfers between devices  7.46 us (13%)
  between operations  1.55 us (3%)
    pallas_call x3, Pallas kernels, run_chunk(): pl.pallas_call(functools.partial(chunk_kernel, spec), out_shape=tuple(out...  30.2 us
    ppermute x9, starting transfers between devices, exchange(): return lax.ppermute(block, 'mp', [(i, i ^ shift) for i in range(ways)])  7.78 us
    ppermute x2, waiting for transfers between devices, body(): came_pooled.append(lax.ppermute(pooled, ('seq', 'mp'), pairs))  5.48 us
    pallas_call x2, Pallas kernels, send_blocks(): pl.pallas_call(functools.partial(send_kernel, quarter, wanted), out_shape...  3.91 us
    ppermute x1, starting transfers between devices, body(): lax.ppermute(blocks[-2], 'seq', [((i + 1) % seq_ways, i) for i in range(s...  3.85 us
    pallas_call x1, Pallas kernels, body(): pl.pallas_call(place_kernel, out_shape=jax.ShapeDtypeStruct(shape, BF), i...  2.29 us
    ppermute x1, waiting for transfers between devices, body(): lax.ppermute(blocks[-1], 'seq', [(i, (i + 1) % seq_ways) for i in range(s...  1.95 us
    pallas_call x1, Pallas kernels, body(): pl.pallas_call(final_kernel, out_shape=jax.ShapeDtypeStruct(shape, BF), i...  1.37 us
  transfers between devices with their start and end apart: 13, of which 2 were waited for; matrix products, arithmetic and copies ran while one was open for 0% of the time, Pallas kernels for 58%

profile of v2, /device:TPU:0, one launch (start us, length us, event | category | flops | bytes accessed | tf_op | source)
XLA Modules:
  0.0 59.1 jit_solution(538420970553296984)
XLA Ops:
  0.6 1.8 %first_blocks.1 = (bf16[64,1024]{1,0:T(8,128)(2,1)}, bf16[64,1024]{1,0:T(8,128)(2,1)}, bf16[64,1024]{1,0:T(8,128)(2,1)}, bf16[64,128]{1,0:T(8,128)(2,1)}, bf16[64,128]{1,0:T(8,128)(2,1)}) custom-call(s32[1]{0:T(128)} %bitcast.mp_ref.refs_0_, bf16[64,16384]{1,0:T(8,128)(2,1)} %bitcast.3), custom_call_target="tpu_custom_call" | custom-call | tf_op jit(solution)/shard_map/first_blocks/pallas_call | solution.py:149
  2.4 2.4 %collective-permute-start = (bf16[64,1024]{1,0:T(8,128)(2,1)}, bf16[64,1024]{1,0:T(8,128)(2,1)S(1)}, u32[]{:S(2)}, u32[]{:S(2)}) collective-permute-start(bf16[64,1024]{1,0:T(8,128)(2,1)} %get-tuple-element.23), channel_id=1, source_target_pairs={{0,3},{1,2},{2,1},{3,0},{4,7},{5,6},{6,5},{7,4},{8,11},{9,10},{10,... | collective-permute-start | bytes 393224 | tf_op jit(solution)/shard_map/ppermute | solution.py:500
  4.9 0.6 %collective-permute-start.1 = (bf16[64,1024]{1,0:T(8,128)(2,1)}, bf16[64,1024]{1,0:T(8,128)(2,1)S(1)}, u32[]{:S(2)}, u32[]{:S(2)}) collective-permute-start(bf16[64,1024]{1,0:T(8,128)(2,1)} %get-tuple-element.24), channel_id=1, source_target_pairs={{0,2},{1,3},{2,0},{3,1},{4,6},{5,7},{6,4},{7,5},{8,10},{9,11},{10,... | collective-permute-start | bytes 393224 | tf_op jit(solution)/shard_map/ppermute | solution.py:500
  5.5 0.0 collective-permute-start.2
  5.5 3.9 %collective-permute-start.3 = (bf16[64,128]{1,0:T(8,128)(2,1)}, bf16[64,128]{1,0:T(8,128)(2,1)S(1)}, u32[]{:S(2)}, u32[]{:S(2)}) collective-permute-start(bf16[64,128]{1,0:T(8,128)(2,1)} %get-tuple-element.26), channel_id=1, source_target_pairs={{4,0},{8,4},{12,8},{0,12},{5,1},{9,5},{13,9},{1,13},{6,2},{10,6},{... | collective-permute-start | bytes 49160 | tf_op jit(solution)/shard_map/ppermute | solution.py:505
  9.4 0.0 collective-permute-start.4
  9.4 2.1 %later_blocks.1 = (bf16[64,1664]{1,0:T(8,128)(2,1)}, bf16[64,1664]{1,0:T(8,128)(2,1)}, bf16[64,1664]{1,0:T(8,128)(2,1)}, bf16[64,1536]{1,0:T(8,128)(2,1)}, bf16[...) custom-call(s32[1]{0:T(128)} %bitcast.mp_ref.refs_0_, bf16[64,16384]{1,0:T(8,128)(2,1)} %bitcast.4), custom_call_target="tpu_custom_call" | custom-call | tf_op jit(solution)/shard_map/later_blocks/pallas_call | solution.py:149
  12.2 0.0 collective-permute-done.3.refs_6_
  12.2 1.0 %collective-permute-start.8 = (bf16[64,1664]{1,0:T(8,128)(2,1)}, bf16[64,1664]{1,0:T(8,128)(2,1)S(1)}, u32[]{:S(2)}, u32[]{:S(2)}) collective-permute-start(bf16[64,1664]{1,0:T(8,128)(2,1)} %get-tuple-element.34), channel_id=1, source_target_pairs={{0,3},{1,2},{2,1},{3,0},{4,7},{5,6},{6,5},{7,4},{8,11},{9,10},{10,... | collective-permute-start | bytes 638984 | tf_op jit(solution)/shard_map/ppermute | solution.py:500
  13.2 2.0 %collective-permute-done.4.refs_7_ = bf16[64,128]{1,0:T(8,128)(2,1)S(1)} collective-permute-done((bf16[64,128]{1,0:T(8,128)(2,1)}, bf16[64,128]{1,0:T(8,128)(2,1)S(1)}, u32[]{:S(2)}, u32[]{:S(2)}) %collective-permute-start.4) | collective-permute-done | bytes 16416 | tf_op jit(solution)/shard_map/ppermute | solution.py:506
  15.1 1.5 %collective-permute-start.9 = (bf16[64,1664]{1,0:T(8,128)(2,1)}, bf16[64,1664]{1,0:T(8,128)(2,1)S(1)}, u32[]{:S(2)}, u32[]{:S(2)}) collective-permute-start(bf16[64,1664]{1,0:T(8,128)(2,1)} %get-tuple-element.35), channel_id=1, source_target_pairs={{0,2},{1,3},{2,0},{3,1},{4,6},{5,7},{6,4},{7,5},{8,10},{9,11},{10,... | collective-permute-start | bytes 638984 | tf_op jit(solution)/shard_map/ppermute | solution.py:500
  16.6 0.0 collective-permute-done.refs_3_.refs_6_.refs_10_
  16.6 0.0 collective-permute-start.10
  16.6 0.0 collective-permute-done.1.refs_4_.refs_7_.refs_11_
  16.6 0.0 collective-permute-done.2.refs_5_.refs_8_.refs_12_
  16.7 8.3 %layer_chunk_1.1 = (bf16[4096,256]{1,0:T(8,128)(2,1)}, bf16[14,8,512]{2,1,0:T(8,128)(2,1)S(1)}, bf16[64,1536]{1,0:T(8,128)(2,1)}, bf16[64,1536]{1,0:T(8,128)(2,1...) custom-call(s32[1]{0:T(128)} %bitcast.mp_ref.refs_0_, ...), custom_call_target="tpu_custom_call", output_to_operand_aliasing={{2}: (8, {}), {3}: (9, {}), {4}: (10, {})} | custom-call | flops 3053453312 | bytes 5111808 | tf_op jit(solution)/shard_map/layer_chunk_1/pallas_call | solution.py:373
  25.0 0.7 %collective-permute-start.5 = (bf16[64,1536]{1,0:T(8,128)(2,1)}, bf16[64,1536]{1,0:T(8,128)(2,1)S(1)}, u32[]{:S(2)}, u32[]{:S(2)}) collective-permute-start(bf16[64,1536]{1,0:T(8,128)(2,1)} %get-tuple-element.31), channel_id=1, source_target_pairs={{0,3},{1,2},{2,1},{3,0},{4,7},{5,6},{6,5},{7,4},{8,11},{9,10},{10,... | collective-permute-start | bytes 589832 | tf_op jit(solution)/shard_map/ppermute | solution.py:500
  25.7 1.5 %collective-permute-start.6 = (bf16[64,1536]{1,0:T(8,128)(2,1)}, bf16[64,1536]{1,0:T(8,128)(2,1)S(1)}, u32[]{:S(2)}, u32[]{:S(2)}) collective-permute-start(bf16[64,1536]{1,0:T(8,128)(2,1)} %get-tuple-element.32), channel_id=1, source_target_pairs={{0,2},{1,3},{2,0},{3,1},{4,6},{5,7},{6,4},{7,5},{8,10},{9,11},{10,... | collective-permute-start | bytes 589832 | tf_op jit(solution)/shard_map/ppermute | solution.py:500
  27.2 0.0 collective-permute-done.8.refs_3_.refs_6_
  27.2 0.0 collective-permute-start.7
  27.2 0.0 collective-permute-done.9.refs_4_.refs_7_
  27.2 0.0 collective-permute-done.10.refs_5_.refs_8_
  27.2 11.0 %layer_chunk_8.1 = (bf16[4096,256]{1,0:T(8,128)(2,1)}, bf16[41,8,512]{2,1,0:T(8,128)(2,1)S(1)}) custom-call(s32[1]{0:T(128)} %bitcast.mp_ref.refs_0_, s32[1]{0:T(128)S(6)} %copy.23.refs_1_.kept_ref, bf16[64,16384]{1,0:T(8,128)(2,1)} %bitcast.6, bf16[64,1664]{1,0:T(8,128)(2,1)S(1)} %collective-permute-done.8.refs_3_.refs_6_, ...), custom_call_target="tpu_custom_call", output_to_operand_aliasing={{0}: (17, {})} | custom-call | flops 5670699008 | bytes 5898240 | tf_op jit(solution)/shard_map/layer_chunk_8/pallas_call | solution.py:373
  38.2 0.5 collective-permute-start.12
  38.7 0.0 collective-permute-done.5.refs_3_
  38.7 0.0 collective-permute-done.6.refs_4_
  38.7 0.0 collective-permute-done.7.refs_5_
  38.7 10.8 %layer_chunk_21.1 = (bf16[4096,256]{1,0:T(8,128)(2,1)}, bf16[26,8,512]{2,1,0:T(8,128)(2,1)S(1)}) custom-call(s32[1]{0:T(128)} %bitcast.mp_ref.refs_0_, s32[1]{0:T(128)S(6)} %copy.23.refs_1_.kept_ref, bf16[64,16384]{1,0:T(8,128)(2,1)} %bitcast.7, bf16[64,1536]{1,0:T(8,128)(2,1)S(1)} %collective-permute-done.5.refs_3_, ...), custom_call_target="tpu_custom_call", output_to_operand_aliasing={{0}: (20, {})} | custom-call | flops 5670699008 | bytes 5898240 | tf_op jit(solution)/shard_map/layer_chunk_21/pallas_call | solution.py:373
  49.6 0.2 collective-permute-start.11
  49.8 0.0 collective-permute-done.12.refs_2_.mark
  49.8 2.3 %place_tiles.1._ = bf16[128,8,512]{2,1,0:T(8,128)(2,1)} custom-call(s32[1]{0:T(128)S(6)} %copy.23.refs_1_.kept_ref, bf16[41,8,512]{2,1,0:T(8,128)(2,1)S(1)} %get-tuple-element.43.refs_0_, bf16[26,8,512]{2,1,0:T(8,128)(2,1)S(1)} %get-tuple-element.42.refs_1_, bf16[41,8,512]{2,1,0:T(8,128)(2,1)S(1)} %collective-permute-done.12.refs_2_.mark), custom_call_target="tpu_custom_call" | custom-call | tf_op jit(solution)/shard_map/place_tiles/pallas_call | solution.py:550
  52.1 5.5 %collective-permute-done.11.piece = bf16[26,8,512]{2,1,0:T(8,128)(2,1)S(1)} collective-permute-done((bf16[26,8,512]{2,1,0:T(8,128)(2,1)S(1)}, bf16[26,8,512]{2,1,0:T(8,128)(2,1)S(1)}, u32[]{:S(2)}, u32[]{:S(2)}) %collective-permute-start.11) | collective-permute-done | bytes 213024 | tf_op jit(solution)/shard_map/ppermute | solution.py:538
  57.6 1.4 %place_final.1 = bf16[128,8,512]{2,1,0:T(8,128)(2,1)} custom-call(s32[1]{0:T(128)S(6)} %copy.23.refs_1_.kept_ref, bf16[26,8,512]{2,1,0:T(8,128)(2,1)S(1)} %collective-permute-done.11.piece, bf16[41,8,512]{2,1,0:T(8,128)(2,1)S(1)} %collective-permute-done.12.refs_2_.mark, bf16[128,8,512]{2,1,0:T(8,128)(2,1)} %place_tiles.1._), custom_call_target="tpu_custom_call", output_to_operand_aliasing={{}: (3, {})} | custom-call | tf_op jit(solution)/shard_map/place_final/pallas_call | solution.py:560
Async XLA Ops:
  2.4 14.2 %collective-permute-start = (bf16[64,1024]{1,0:T(8,128)(2,1)}, bf16[64,1024]{1,0:T(8,128)(2,1)S(1)}, u32[]{:S(2)}, u32[]{:S(2)}) collective-permute-start(bf16[64,1024]{1,0:T(8,128)(2,1)} %get-tuple-element.23), channel_id=1, source_target_pairs={{0,3},{1,2},{2,1},{3,0},{4,7},{5,6},{6,5},{7,4},{8,11},{9,10},{10,... | collective-permute-start | bytes 393224 | tf_op jit(solution)/shard_map/ppermute | solution.py:500
  4.9 11.8 %collective-permute-start.1 = (bf16[64,1024]{1,0:T(8,128)(2,1)}, bf16[64,1024]{1,0:T(8,128)(2,1)S(1)}, u32[]{:S(2)}, u32[]{:S(2)}) collective-permute-start(bf16[64,1024]{1,0:T(8,128)(2,1)} %get-tuple-element.24), channel_id=1, source_target_pairs={{0,2},{1,3},{2,0},{3,1},{4,6},{5,7},{6,4},{7,5},{8,10},{9,11},{10,... | collective-permute-start | bytes 393224 | tf_op jit(solution)/shard_map/ppermute | solution.py:500
  5.5 11.1 %collective-permute-start.2 = (bf16[64,1024]{1,0:T(8,128)(2,1)}, bf16[64,1024]{1,0:T(8,128)(2,1)S(1)}, u32[]{:S(2)}, u32[]{:S(2)}) collective-permute-start(bf16[64,1024]{1,0:T(8,128)(2,1)} %get-tuple-element.25), channel_id=1, source_target_pairs={{0,1},{1,0},{2,3},{3,2},{4,5},{5,4},{6,7},{7,6},{8,9},{9,8},{10,11... | collective-permute-start | bytes 393224 | tf_op jit(solution)/shard_map/ppermute | solution.py:500
  5.5 6.6 %collective-permute-start.3 = (bf16[64,128]{1,0:T(8,128)(2,1)}, bf16[64,128]{1,0:T(8,128)(2,1)S(1)}, u32[]{:S(2)}, u32[]{:S(2)}) collective-permute-start(bf16[64,128]{1,0:T(8,128)(2,1)} %get-tuple-element.26), channel_id=1, source_target_pairs={{4,0},{8,4},{12,8},{0,12},{5,1},{9,5},{13,9},{1,13},{6,2},{10,6},{... | collective-permute-start | bytes 49160 | tf_op jit(solution)/shard_map/ppermute | solution.py:505
  9.4 5.7 %collective-permute-start.4 = (bf16[64,128]{1,0:T(8,128)(2,1)}, bf16[64,128]{1,0:T(8,128)(2,1)S(1)}, u32[]{:S(2)}, u32[]{:S(2)}) collective-permute-start(bf16[64,128]{1,0:T(8,128)(2,1)} %get-tuple-element.27), channel_id=1, source_target_pairs={{0,4},{4,8},{8,12},{12,0},{1,5},{5,9},{9,13},{13,1},{2,6},{6,10},{... | collective-permute-start | bytes 49160 | tf_op jit(solution)/shard_map/ppermute | solution.py:506
  12.2 15.0 %collective-permute-start.8 = (bf16[64,1664]{1,0:T(8,128)(2,1)}, bf16[64,1664]{1,0:T(8,128)(2,1)S(1)}, u32[]{:S(2)}, u32[]{:S(2)}) collective-permute-start(bf16[64,1664]{1,0:T(8,128)(2,1)} %get-tuple-element.34), channel_id=1, source_target_pairs={{0,3},{1,2},{2,1},{3,0},{4,7},{5,6},{6,5},{7,4},{8,11},{9,10},{10,... | collective-permute-start | bytes 638984 | tf_op jit(solution)/shard_map/ppermute | solution.py:500
  15.1 12.0 %collective-permute-start.9 = (bf16[64,1664]{1,0:T(8,128)(2,1)}, bf16[64,1664]{1,0:T(8,128)(2,1)S(1)}, u32[]{:S(2)}, u32[]{:S(2)}) collective-permute-start(bf16[64,1664]{1,0:T(8,128)(2,1)} %get-tuple-element.35), channel_id=1, source_target_pairs={{0,2},{1,3},{2,0},{3,1},{4,6},{5,7},{6,4},{7,5},{8,10},{9,11},{10,... | collective-permute-start | bytes 638984 | tf_op jit(solution)/shard_map/ppermute | solution.py:500
  16.6 10.6 %collective-permute-start.10 = (bf16[64,1664]{1,0:T(8,128)(2,1)}, bf16[64,1664]{1,0:T(8,128)(2,1)S(1)}, u32[]{:S(2)}, u32[]{:S(2)}) collective-permute-start(bf16[64,1664]{1,0:T(8,128)(2,1)} %get-tuple-element.36), channel_id=1, source_target_pairs={{0,1},{1,0},{2,3},{3,2},{4,5},{5,4},{6,7},{7,6},{8,9},{9,8},{10,11... | collective-permute-start | bytes 638984 | tf_op jit(solution)/shard_map/ppermute | solution.py:500
  25.0 13.7 %collective-permute-start.5 = (bf16[64,1536]{1,0:T(8,128)(2,1)}, bf16[64,1536]{1,0:T(8,128)(2,1)S(1)}, u32[]{:S(2)}, u32[]{:S(2)}) collective-permute-start(bf16[64,1536]{1,0:T(8,128)(2,1)} %get-tuple-element.31), channel_id=1, source_target_pairs={{0,3},{1,2},{2,1},{3,0},{4,7},{5,6},{6,5},{7,4},{8,11},{9,10},{10,... | collective-permute-start | bytes 589832 | tf_op jit(solution)/shard_map/ppermute | solution.py:500
  25.7 13.0 %collective-permute-start.6 = (bf16[64,1536]{1,0:T(8,128)(2,1)}, bf16[64,1536]{1,0:T(8,128)(2,1)S(1)}, u32[]{:S(2)}, u32[]{:S(2)}) collective-permute-start(bf16[64,1536]{1,0:T(8,128)(2,1)} %get-tuple-element.32), channel_id=1, source_target_pairs={{0,2},{1,3},{2,0},{3,1},{4,6},{5,7},{6,4},{7,5},{8,10},{9,11},{10,... | collective-permute-start | bytes 589832 | tf_op jit(solution)/shard_map/ppermute | solution.py:500
  27.2 11.6 %collective-permute-start.7 = (bf16[64,1536]{1,0:T(8,128)(2,1)}, bf16[64,1536]{1,0:T(8,128)(2,1)S(1)}, u32[]{:S(2)}, u32[]{:S(2)}) collective-permute-start(bf16[64,1536]{1,0:T(8,128)(2,1)} %get-tuple-element.33), channel_id=1, source_target_pairs={{0,1},{1,0},{2,3},{3,2},{4,5},{5,4},{6,7},{7,6},{8,9},{9,8},{10,11... | collective-permute-start | bytes 589832 | tf_op jit(solution)/shard_map/ppermute | solution.py:500
  38.2 11.6 %collective-permute-start.12 = (bf16[41,8,512]{2,1,0:T(8,128)(2,1)S(1)}, bf16[41,8,512]{2,1,0:T(8,128)(2,1)S(1)}, u32[]{:S(2)}, u32[]{:S(2)}) collective-permute-start(bf16[41,8,512]{2,1,0:T(8,128)(2,1)S(1)} %get-tuple-element.43.refs_0_), channel_id=1, source_target_pairs={{0,1},{1,2},{2,3},{3,4},{4,5},{5,6},{6,7},{7,8},{8,9},{9,10},{10,1... | collective-permute-start | bytes 1007624 | tf_op jit(solution)/shard_map/ppermute | solution.py:538
  49.6 8.0 %collective-permute-start.11 = (bf16[26,8,512]{2,1,0:T(8,128)(2,1)S(1)}, bf16[26,8,512]{2,1,0:T(8,128)(2,1)S(1)}, u32[]{:S(2)}, u32[]{:S(2)}) collective-permute-start(bf16[26,8,512]{2,1,0:T(8,128)(2,1)S(1)} %get-tuple-element.42.refs_1_), channel_id=1, source_target_pairs={{0,1},{1,2},{2,3},{3,4},{4,5},{5,6},{6,7},{7,8},{8,9},{9,10},{10,1... | collective-permute-start | bytes 638984 | tf_op jit(solution)/shard_map/ppermute | solution.py:538

commit v3 on v2

--- a/solution.py
+++ b/solution.py
@@ -118,7 +118,7 @@
         v = values[rows]
         wide = jnp.concatenate([v[:run]] * HEADS + [v[run:]] * HEADS, axis=0) * mask
         mixed.append(dot_nn(shares[rows], wide))
-    attended = (jnp.concatenate(mixed, axis=0) / total).astype(BF)
+    attended = (jnp.concatenate(mixed, axis=0) * pl.reciprocal(total)).astype(BF)
     arrive(3, 6)
     hidden = x + dot_nn(attended, wo[...])
     return feed_forward(hidden, norm_rows(hidden).astype(BF), wu, wd)
@@ -500,10 +500,10 @@
         return lax.ppermute(block, "mp", [(i, i ^ shift) for i in range(ways)])
 
     edges = [(None, 0, 1, 0), (None, own.shape[1] // BLOCK - 1, 1, 0)]
-    blocks = send_blocks(mp_index, own, quarter, [(s, *spans[0], 0) for s in SHIFTS] + edges, "first_blocks")
+    blocks = send_blocks(mp_index, own, quarter, [(s, *spans[0], 0) for s in SHIFTS], "first_blocks")
     received = [[exchange(b, s) for b, s in zip(blocks, SHIFTS)]]
-    after = lax.ppermute(blocks[-2], "seq", [((i + 1) % seq_ways, i) for i in range(seq_ways)])
-    prior = lax.ppermute(blocks[-1], "seq", [(i, (i + 1) % seq_ways) for i in range(seq_ways)])
+    after = lax.ppermute(own[:, :BLOCK], "seq", [((i + 1) % seq_ways, i) for i in range(seq_ways)])
+    prior = lax.ppermute(own[:, own.shape[1] - BLOCK :], "seq", [(i, (i + 1) % seq_ways) for i in range(seq_ways)])
     wanted = [(s, *spans[n], int(n == last_chunk)) for n in range(1, last_chunk + 1) for s in SHIFTS]
     blocks = list(send_blocks(mp_index, own, quarter, wanted, "later_blocks"))
     for n in range(last_chunk - 1):

time: 59.1 us -> 57.3 us (0.970)
  waiting for transfers between devices: 7.46 us -> 4.62 us
  local copies, waits for them, and re-layouts: 0 us -> 0.74 us
    ppermute x2, waiting for transfers between devices: 1.95 us -> 0.01 us  [the longest x1 0.01 us: body(): lax.ppermute(own[:, own.shape[1] - BLOCK:], 'seq', [(i, (i + 1) % seq_way...]
    ppermute x2, starting transfers between devices: 0.76 us -> 1.66 us  [body(): came_pooled.append(lax.ppermute(pooled, ('seq', 'mp'), pairs))]
    ppermute x2, waiting for transfers between devices: 5.48 us -> 4.59 us  [body(): came_pooled.append(lax.ppermute(pooled, ('seq', 'mp'), pairs))]
    slice x0 -> x1, local copies, waits for them, and re-layouts: none -> 0.74 us  [body(): own[:, own.shape[1] - BLOCK:]]
  transfers between devices with their start and end apart: 13 -> 13, of which waited for: 2 -> 1; matrix products, arithmetic and copies ran while one was open for 0% -> 1% of each run, Pallas kernels for 58% -> 60%
where the time goes in v3:
time: 57.3 us
  Pallas kernels  37.7 us (66%)
  starting transfers between devices  12.7 us (22%)
  waiting for transfers between devices  4.62 us (8%)
  between operations  1.54 us (3%)
  local copies, waits for them, and re-layouts  0.74 us (1%)
    pallas_call x3, Pallas kernels, run_chunk(): pl.pallas_call(functools.partial(chunk_kernel, spec), out_shape=tuple(out...  30.2 us
    ppermute x9, starting transfers between devices, exchange(): return lax.ppermute(block, 'mp', [(i, i ^ shift) for i in range(ways)])  7.21 us
    ppermute x2, waiting for transfers between devices, body(): came_pooled.append(lax.ppermute(pooled, ('seq', 'mp'), pairs))  4.59 us
    pallas_call x2, Pallas kernels, send_blocks(): pl.pallas_call(functools.partial(send_kernel, quarter, wanted), out_shape...  3.89 us
    pallas_call x1, Pallas kernels, body(): pl.pallas_call(place_kernel, out_shape=jax.ShapeDtypeStruct(shape, BF), i...  2.3 us
    ppermute x1, starting transfers between devices, body(): lax.ppermute(own[:, :BLOCK], 'seq', [((i + 1) % seq_ways, i) for i in ran...  2.03 us
    ppermute x1, starting transfers between devices, body(): lax.ppermute(own[:, own.shape[1] - BLOCK:], 'seq', [(i, (i + 1) % seq_way...  1.83 us
    ppermute x2, starting transfers between devices, body(): came_pooled.append(lax.ppermute(pooled, ('seq', 'mp'), pairs))  1.66 us
  transfers between devices with their start and end apart: 13, of which 1 were waited for; matrix products, arithmetic and copies ran while one was open for 1% of the time, Pallas kernels for 60%

profile of v3, /device:TPU:0, one launch (start us, length us, event | category | flops | bytes accessed | tf_op | source)
XLA Modules:
  0.0 57.3 jit_solution(6550225407569617429)
XLA Ops:
  0.6 1.8 %first_blocks.1 = (bf16[64,1024]{1,0:T(8,128)(2,1)}, bf16[64,1024]{1,0:T(8,128)(2,1)}, bf16[64,1024]{1,0:T(8,128)(2,1)}) custom-call(s32[1]{0:T(128)} %bitcast.mp_ref.refs_0_, bf16[64,16384]{1,0:T(8,128)(2,1)} %bitcast.3), custom_call_target="tpu_custom_call" | custom-call | tf_op jit(solution)/shard_map/first_blocks/pallas_call | solution.py:149
  2.4 2.4 %collective-permute-start = (bf16[64,1024]{1,0:T(8,128)(2,1)}, bf16[64,1024]{1,0:T(8,128)(2,1)S(1)}, u32[]{:S(2)}, u32[]{:S(2)}) collective-permute-start(bf16[64,1024]{1,0:T(8,128)(2,1)} %get-tuple-element.21), channel_id=1, source_target_pairs={{0,3},{1,2},{2,1},{3,0},{4,7},{5,6},{6,5},{7,4},{8,11},{9,10},{10,... | collective-permute-start | bytes 393224 | tf_op jit(solution)/shard_map/ppermute | solution.py:500
  4.8 0.6 %collective-permute-start.1 = (bf16[64,1024]{1,0:T(8,128)(2,1)}, bf16[64,1024]{1,0:T(8,128)(2,1)S(1)}, u32[]{:S(2)}, u32[]{:S(2)}) collective-permute-start(bf16[64,1024]{1,0:T(8,128)(2,1)} %get-tuple-element.22), channel_id=1, source_target_pairs={{0,2},{1,3},{2,0},{3,1},{4,6},{5,7},{6,4},{7,5},{8,10},{9,11},{10,... | collective-permute-start | bytes 393224 | tf_op jit(solution)/shard_map/ppermute | solution.py:500
  5.5 0.0 collective-permute-start.2
  5.5 0.7 %fusion = (bf16[64,128]{1,0:T(8,128)(2,1)S(1)}, bf16[64,128]{1,0:T(8,128)(2,1)S(1)}) fusion(bf16[64,16384]{1,0:T(8,128)(2,1)} %bitcast.4), kind=kLoop, calls=%fused_computation | loop fusion | bytes 65536 | tf_op jit(solution)/shard_map/slice | solution.py:506
  6.3 1.8 %collective-permute-start.4 = (bf16[64,128]{1,0:T(8,128)(2,1)S(1)}, bf16[64,128]{1,0:T(8,128)(2,1)S(1)}, u32[]{:S(2)}, u32[]{:S(2)}) collective-permute-start(bf16[64,128]{1,0:T(8,128)(2,1)S(1)} %get-tuple-element.40), channel_id=1, source_target_pairs={{0,4},{4,8},{8,12},{12,0},{1,5},{5,9},{9,13},{13,1},{2,6},{6,10},{... | collective-permute-start | bytes 49160 | tf_op jit(solution)/shard_map/ppermute | solution.py:506
  8.1 2.0 %collective-permute-start.3 = (bf16[64,128]{1,0:T(8,128)(2,1)S(1)}, bf16[64,128]{1,0:T(8,128)(2,1)S(1)}, u32[]{:S(2)}, u32[]{:S(2)}) collective-permute-start(bf16[64,128]{1,0:T(8,128)(2,1)S(1)} %get-tuple-element.41), channel_id=1, source_target_pairs={{4,0},{8,4},{12,8},{0,12},{5,1},{9,5},{13,9},{1,13},{6,2},{10,6},{... | collective-permute-start | bytes 49160 | tf_op jit(solution)/shard_map/ppermute | solution.py:505
  10.1 2.1 %later_blocks.1 = (bf16[64,1664]{1,0:T(8,128)(2,1)}, bf16[64,1664]{1,0:T(8,128)(2,1)}, bf16[64,1664]{1,0:T(8,128)(2,1)}, bf16[64,1536]{1,0:T(8,128)(2,1)}, bf16[...) custom-call(s32[1]{0:T(128)} %bitcast.mp_ref.refs_0_, bf16[64,16384]{1,0:T(8,128)(2,1)} %bitcast.5), custom_call_target="tpu_custom_call" | custom-call | tf_op jit(solution)/shard_map/later_blocks/pallas_call | solution.py:149
  12.9 0.0 collective-permute-done.4.refs_7_
  12.9 1.0 %collective-permute-start.8 = (bf16[64,1664]{1,0:T(8,128)(2,1)}, bf16[64,1664]{1,0:T(8,128)(2,1)S(1)}, u32[]{:S(2)}, u32[]{:S(2)}) collective-permute-start(bf16[64,1664]{1,0:T(8,128)(2,1)} %get-tuple-element.30), channel_id=1, source_target_pairs={{0,3},{1,2},{2,1},{3,0},{4,7},{5,6},{6,5},{7,4},{8,11},{9,10},{10,... | collective-permute-start | bytes 638984 | tf_op jit(solution)/shard_map/ppermute | solution.py:500
  13.9 0.0 collective-permute-done.3.refs_6_
  13.9 0.9 %collective-permute-start.9 = (bf16[64,1664]{1,0:T(8,128)(2,1)}, bf16[64,1664]{1,0:T(8,128)(2,1)S(1)}, u32[]{:S(2)}, u32[]{:S(2)}) collective-permute-start(bf16[64,1664]{1,0:T(8,128)(2,1)} %get-tuple-element.31), channel_id=1, source_target_pairs={{0,2},{1,3},{2,0},{3,1},{4,6},{5,7},{6,4},{7,5},{8,10},{9,11},{10,... | collective-permute-start | bytes 638984 | tf_op jit(solution)/shard_map/ppermute | solution.py:500
  14.8 0.0 collective-permute-done.refs_3_.refs_6_.refs_10_
  14.8 0.1 collective-permute-start.10
  14.9 0.0 collective-permute-done.1.refs_4_.refs_7_.refs_11_
  14.9 0.0 collective-permute-done.2.refs_5_.refs_8_.refs_12_
  14.9 8.3 %layer_chunk_1.1 = (bf16[4096,256]{1,0:T(8,128)(2,1)}, bf16[14,8,512]{2,1,0:T(8,128)(2,1)S(1)}, bf16[64,1536]{1,0:T(8,128)(2,1)}, bf16[64,1536]{1,0:T(8,128)(2,1...) custom-call(s32[1]{0:T(128)} %bitcast.mp_ref.refs_0_, ...), custom_call_target="tpu_custom_call", output_to_operand_aliasing={{2}: (8, {}), {3}: (9, {}), {4}: (10, {})} | custom-call | flops 3053453312 | bytes 5111808 | tf_op jit(solution)/shard_map/layer_chunk_1/pallas_call | solution.py:373
  23.2 1.4 %collective-permute-start.5 = (bf16[64,1536]{1,0:T(8,128)(2,1)}, bf16[64,1536]{1,0:T(8,128)(2,1)S(1)}, u32[]{:S(2)}, u32[]{:S(2)}) collective-permute-start(bf16[64,1536]{1,0:T(8,128)(2,1)} %get-tuple-element.27), channel_id=1, source_target_pairs={{0,3},{1,2},{2,1},{3,0},{4,7},{5,6},{6,5},{7,4},{8,11},{9,10},{10,... | collective-permute-start | bytes 589832 | tf_op jit(solution)/shard_map/ppermute | solution.py:500
  24.6 0.7 %collective-permute-start.6 = (bf16[64,1536]{1,0:T(8,128)(2,1)}, bf16[64,1536]{1,0:T(8,128)(2,1)S(1)}, u32[]{:S(2)}, u32[]{:S(2)}) collective-permute-start(bf16[64,1536]{1,0:T(8,128)(2,1)} %get-tuple-element.28), channel_id=1, source_target_pairs={{0,2},{1,3},{2,0},{3,1},{4,6},{5,7},{6,4},{7,5},{8,10},{9,11},{10,... | collective-permute-start | bytes 589832 | tf_op jit(solution)/shard_map/ppermute | solution.py:500
  25.3 0.0 collective-permute-done.8.refs_3_.refs_6_
  25.3 0.0 collective-permute-start.7
  25.4 0.0 collective-permute-done.9.refs_4_.refs_7_
  25.4 0.0 collective-permute-done.10.refs_5_.refs_8_
  25.4 11.0 %layer_chunk_8.1 = (bf16[4096,256]{1,0:T(8,128)(2,1)}, bf16[41,8,512]{2,1,0:T(8,128)(2,1)S(1)}) custom-call(s32[1]{0:T(128)} %bitcast.mp_ref.refs_0_, s32[1]{0:T(128)S(6)} %copy.23.refs_1_.kept_ref, bf16[64,16384]{1,0:T(8,128)(2,1)} %bitcast.7, bf16[64,1664]{1,0:T(8,128)(2,1)S(1)} %collective-permute-done.8.refs_3_.refs_6_, ...), custom_call_target="tpu_custom_call", output_to_operand_aliasing={{0}: (17, {})} | custom-call | flops 5670699008 | bytes 5898240 | tf_op jit(solution)/shard_map/layer_chunk_8/pallas_call | solution.py:373
  36.4 0.5 collective-permute-start.12
  36.9 0.0 collective-permute-done.5.refs_3_
  36.9 0.0 collective-permute-done.6.refs_4_
  36.9 0.0 collective-permute-done.7.refs_5_
  36.9 10.8 %layer_chunk_21.1 = (bf16[4096,256]{1,0:T(8,128)(2,1)}, bf16[26,8,512]{2,1,0:T(8,128)(2,1)S(1)}) custom-call(s32[1]{0:T(128)} %bitcast.mp_ref.refs_0_, s32[1]{0:T(128)S(6)} %copy.23.refs_1_.kept_ref, bf16[64,16384]{1,0:T(8,128)(2,1)} %bitcast.8, bf16[64,1536]{1,0:T(8,128)(2,1)S(1)} %collective-permute-done.5.refs_3_, ...), custom_call_target="tpu_custom_call", output_to_operand_aliasing={{0}: (20, {})} | custom-call | flops 5670699008 | bytes 5898240 | tf_op jit(solution)/shard_map/layer_chunk_21/pallas_call | solution.py:373
  47.8 1.1 %collective-permute-start.11 = (bf16[26,8,512]{2,1,0:T(8,128)(2,1)S(1)}, bf16[26,8,512]{2,1,0:T(8,128)(2,1)S(1)}, u32[]{:S(2)}, u32[]{:S(2)}) collective-permute-start(bf16[26,8,512]{2,1,0:T(8,128)(2,1)S(1)} %get-tuple-element.38.refs_1_), channel_id=1, source_target_pairs={{0,1},{1,2},{2,3},{3,4},{4,5},{5,6},{6,7},{7,8},{8,9},{9,10},{10,1... | collective-permute-start | bytes 638984 | tf_op jit(solution)/shard_map/ppermute | solution.py:538
  48.9 0.0 collective-permute-done.12.refs_2_.mark
  48.9 2.3 %place_tiles.1._ = bf16[128,8,512]{2,1,0:T(8,128)(2,1)} custom-call(s32[1]{0:T(128)S(6)} %copy.23.refs_1_.kept_ref, bf16[41,8,512]{2,1,0:T(8,128)(2,1)S(1)} %get-tuple-element.39.refs_0_, bf16[26,8,512]{2,1,0:T(8,128)(2,1)S(1)} %get-tuple-element.38.refs_1_, bf16[41,8,512]{2,1,0:T(8,128)(2,1)S(1)} %collective-permute-done.12.refs_2_.mark), custom_call_target="tpu_custom_call" | custom-call | tf_op jit(solution)/shard_map/place_tiles/pallas_call | solution.py:550
  51.2 4.6 %collective-permute-done.11.piece = bf16[26,8,512]{2,1,0:T(8,128)(2,1)S(1)} collective-permute-done((bf16[26,8,512]{2,1,0:T(8,128)(2,1)S(1)}, bf16[26,8,512]{2,1,0:T(8,128)(2,1)S(1)}, u32[]{:S(2)}, u32[]{:S(2)}) %collective-permute-start.11) | collective-permute-done | bytes 213024 | tf_op jit(solution)/shard_map/ppermute | solution.py:538
  55.8 1.3 %place_final.1 = bf16[128,8,512]{2,1,0:T(8,128)(2,1)} custom-call(s32[1]{0:T(128)S(6)} %copy.23.refs_1_.kept_ref, bf16[26,8,512]{2,1,0:T(8,128)(2,1)S(1)} %collective-permute-done.11.piece, bf16[41,8,512]{2,1,0:T(8,128)(2,1)S(1)} %collective-permute-done.12.refs_2_.mark, bf16[128,8,512]{2,1,0:T(8,128)(2,1)} %place_tiles.1._), custom_call_target="tpu_custom_call", output_to_operand_aliasing={{}: (3, {})} | custom-call | tf_op jit(solution)/shard_map/place_final/pallas_call | solution.py:560
Async XLA Ops:
  2.4 12.4 %collective-permute-start = (bf16[64,1024]{1,0:T(8,128)(2,1)}, bf16[64,1024]{1,0:T(8,128)(2,1)S(1)}, u32[]{:S(2)}, u32[]{:S(2)}) collective-permute-start(bf16[64,1024]{1,0:T(8,128)(2,1)} %get-tuple-element.21), channel_id=1, source_target_pairs={{0,3},{1,2},{2,1},{3,0},{4,7},{5,6},{6,5},{7,4},{8,11},{9,10},{10,... | collective-permute-start | bytes 393224 | tf_op jit(solution)/shard_map/ppermute | solution.py:500
  4.8 10.0 %collective-permute-start.1 = (bf16[64,1024]{1,0:T(8,128)(2,1)}, bf16[64,1024]{1,0:T(8,128)(2,1)S(1)}, u32[]{:S(2)}, u32[]{:S(2)}) collective-permute-start(bf16[64,1024]{1,0:T(8,128)(2,1)} %get-tuple-element.22), channel_id=1, source_target_pairs={{0,2},{1,3},{2,0},{3,1},{4,6},{5,7},{6,4},{7,5},{8,10},{9,11},{10,... | collective-permute-start | bytes 393224 | tf_op jit(solution)/shard_map/ppermute | solution.py:500
  5.5 9.4 %collective-permute-start.2 = (bf16[64,1024]{1,0:T(8,128)(2,1)}, bf16[64,1024]{1,0:T(8,128)(2,1)S(1)}, u32[]{:S(2)}, u32[]{:S(2)}) collective-permute-start(bf16[64,1024]{1,0:T(8,128)(2,1)} %get-tuple-element.23), channel_id=1, source_target_pairs={{0,1},{1,0},{2,3},{3,2},{4,5},{5,4},{6,7},{7,6},{8,9},{9,8},{10,11... | collective-permute-start | bytes 393224 | tf_op jit(solution)/shard_map/ppermute | solution.py:500
  6.3 6.7 %collective-permute-start.4 = (bf16[64,128]{1,0:T(8,128)(2,1)S(1)}, bf16[64,128]{1,0:T(8,128)(2,1)S(1)}, u32[]{:S(2)}, u32[]{:S(2)}) collective-permute-start(bf16[64,128]{1,0:T(8,128)(2,1)S(1)} %get-tuple-element.40), channel_id=1, source_target_pairs={{0,4},{4,8},{8,12},{12,0},{1,5},{5,9},{9,13},{13,1},{2,6},{6,10},{... | collective-permute-start | bytes 49160 | tf_op jit(solution)/shard_map/ppermute | solution.py:506
  8.1 5.8 %collective-permute-start.3 = (bf16[64,128]{1,0:T(8,128)(2,1)S(1)}, bf16[64,128]{1,0:T(8,128)(2,1)S(1)}, u32[]{:S(2)}, u32[]{:S(2)}) collective-permute-start(bf16[64,128]{1,0:T(8,128)(2,1)S(1)} %get-tuple-element.41), channel_id=1, source_target_pairs={{4,0},{8,4},{12,8},{0,12},{5,1},{9,5},{13,9},{1,13},{6,2},{10,6},{... | collective-permute-start | bytes 49160 | tf_op jit(solution)/shard_map/ppermute | solution.py:505
  12.9 12.4 %collective-permute-start.8 = (bf16[64,1664]{1,0:T(8,128)(2,1)}, bf16[64,1664]{1,0:T(8,128)(2,1)S(1)}, u32[]{:S(2)}, u32[]{:S(2)}) collective-permute-start(bf16[64,1664]{1,0:T(8,128)(2,1)} %get-tuple-element.30), channel_id=1, source_target_pairs={{0,3},{1,2},{2,1},{3,0},{4,7},{5,6},{6,5},{7,4},{8,11},{9,10},{10,... | collective-permute-start | bytes 638984 | tf_op jit(solution)/shard_map/ppermute | solution.py:500
  13.9 11.4 %collective-permute-start.9 = (bf16[64,1664]{1,0:T(8,128)(2,1)}, bf16[64,1664]{1,0:T(8,128)(2,1)S(1)}, u32[]{:S(2)}, u32[]{:S(2)}) collective-permute-start(bf16[64,1664]{1,0:T(8,128)(2,1)} %get-tuple-element.31), channel_id=1, source_target_pairs={{0,2},{1,3},{2,0},{3,1},{4,6},{5,7},{6,4},{7,5},{8,10},{9,11},{10,... | collective-permute-start | bytes 638984 | tf_op jit(solution)/shard_map/ppermute | solution.py:500
  14.8 10.6 %collective-permute-start.10 = (bf16[64,1664]{1,0:T(8,128)(2,1)}, bf16[64,1664]{1,0:T(8,128)(2,1)S(1)}, u32[]{:S(2)}, u32[]{:S(2)}) collective-permute-start(bf16[64,1664]{1,0:T(8,128)(2,1)} %get-tuple-element.32), channel_id=1, source_target_pairs={{0,1},{1,0},{2,3},{3,2},{4,5},{5,4},{6,7},{7,6},{8,9},{9,8},{10,11... | collective-permute-start | bytes 638984 | tf_op jit(solution)/shard_map/ppermute | solution.py:500
  23.2 13.7 %collective-permute-start.5 = (bf16[64,1536]{1,0:T(8,128)(2,1)}, bf16[64,1536]{1,0:T(8,128)(2,1)S(1)}, u32[]{:S(2)}, u32[]{:S(2)}) collective-permute-start(bf16[64,1536]{1,0:T(8,128)(2,1)} %get-tuple-element.27), channel_id=1, source_target_pairs={{0,3},{1,2},{2,1},{3,0},{4,7},{5,6},{6,5},{7,4},{8,11},{9,10},{10,... | collective-permute-start | bytes 589832 | tf_op jit(solution)/shard_map/ppermute | solution.py:500
  24.6 12.3 %collective-permute-start.6 = (bf16[64,1536]{1,0:T(8,128)(2,1)}, bf16[64,1536]{1,0:T(8,128)(2,1)S(1)}, u32[]{:S(2)}, u32[]{:S(2)}) collective-permute-start(bf16[64,1536]{1,0:T(8,128)(2,1)} %get-tuple-element.28), channel_id=1, source_target_pairs={{0,2},{1,3},{2,0},{3,1},{4,6},{5,7},{6,4},{7,5},{8,10},{9,11},{10,... | collective-permute-start | bytes 589832 | tf_op jit(solution)/shard_map/ppermute | solution.py:500
  25.3 11.6 %collective-permute-start.7 = (bf16[64,1536]{1,0:T(8,128)(2,1)}, bf16[64,1536]{1,0:T(8,128)(2,1)S(1)}, u32[]{:S(2)}, u32[]{:S(2)}) collective-permute-start(bf16[64,1536]{1,0:T(8,128)(2,1)} %get-tuple-element.29), channel_id=1, source_target_pairs={{0,1},{1,0},{2,3},{3,2},{4,5},{5,4},{6,7},{7,6},{8,9},{9,8},{10,11... | collective-permute-start | bytes 589832 | tf_op jit(solution)/shard_map/ppermute | solution.py:500
  36.4 12.5 %collective-permute-start.12 = (bf16[41,8,512]{2,1,0:T(8,128)(2,1)S(1)}, bf16[41,8,512]{2,1,0:T(8,128)(2,1)S(1)}, u32[]{:S(2)}, u32[]{:S(2)}) collective-permute-start(bf16[41,8,512]{2,1,0:T(8,128)(2,1)S(1)} %get-tuple-element.39.refs_0_), channel_id=1, source_target_pairs={{0,1},{1,2},{2,3},{3,4},{4,5},{5,6},{6,7},{7,8},{8,9},{9,10},{10,1... | collective-permute-start | bytes 1007624 | tf_op jit(solution)/shard_map/ppermute | solution.py:538
  47.8 8.0 %collective-permute-start.11 = (bf16[26,8,512]{2,1,0:T(8,128)(2,1)S(1)}, bf16[26,8,512]{2,1,0:T(8,128)(2,1)S(1)}, u32[]{:S(2)}, u32[]{:S(2)}) collective-permute-start(bf16[26,8,512]{2,1,0:T(8,128)(2,1)S(1)} %get-tuple-element.38.refs_1_), channel_id=1, source_target_pairs={{0,1},{1,2},{2,3},{3,4},{4,5},{5,6},{6,7},{7,8},{8,9},{9,10},{10,1... | collective-permute-start | bytes 638984 | tf_op jit(solution)/shard_map/ppermute | solution.py:538
